TPU v7x, 512 devices: a whole 4x4x16 slice. The times are simulated.
512 devices in a mesh: mem: 16 (over z_lo, core), lat: 32 (over x, y, z_hi).
Axes of the slice: x: 4, y: 4, z: 16 (z_hi: 2, z_lo: 8; z = z_hi * 8 + z_lo), core: 2. Of those that a mesh axis runs over, the one named last changes fastest.
Arguments:
- control: bfloat16 [32, 10, 704, 1440], P('mem', None, 'lat'), may hold values from -6 to 6
- perturb: bfloat16 [32, 10, 704, 1440], P('mem', None, None, 'lat'), may hold values from -6 to 6
- lon_loc: bfloat16 [1440, 1440], P(None, 'mem'), may hold values from 0 to 1, as said below
- lat_loc: bfloat16 [704, 704], P('mem'), may hold values from 0 to 1, as said below
- static_scale: float32 [10, 704, 1440], P(None, 'mem', 'lat'), may hold values from 0.3 to 1
- static_field: float32 [10, 704, 1440], P(None, 'mem', 'lat'), may hold values from -6 to 6
- courant: float32 [2, 704, 1440], P(None, 'mem', 'lat'), may hold values from -0.48 to 0.48
Outputs:
- increment: float32 [10, 704, 1440], P(None, 'mem', 'lat')
- evolved: float32 [10, 704, 1440], P(None, 'mem', 'lat')
Inputs may be any that keep to these rules, and one draw needn't show every extreme that they name: `lon_loc`: Symmetric, with positive entries. `lat_loc`: Symmetric, with positive entries.
All inputs are finite; a program needn't handle non-finite values.
Results may differ from a plain program's by a relative error of at most 0.0027.
Values may be sent and summed in bfloat16 or wider, within the bound.
A program may use at most 64 MiB of HBM per device.

v0:
```python
import math

import jax
import jax.numpy as jnp
from jax import lax
from jax.sharding import PartitionSpec as P

NLAT = 704
STEPS = 4


def padded_2(shard, sides, width, wrap):
    for axis, dim in sides:
        size, length = (lax.axis_size(axis), shard.shape[dim])
        up = [(i, (i + 1) % size) for i in range(size if wrap else size - 1)]
        down = [(j, i) for i, j in up]
        last = lax.slice_in_dim(shard, length - width, length, axis=dim)
        leading = lax.slice_in_dim(shard, 0, width, axis=dim)
        before = lax.ppermute(last, axis, up)
        after = lax.ppermute(leading, axis, down)
        shard = jnp.concatenate([before, shard, after], axis=dim)
    return shard


def in_order(parts, dim):
    shape = list(parts.shape[1:])
    shape[dim] *= parts.shape[0]
    return jnp.moveaxis(parts, 0, dim).reshape(shape)


def sent_to_all(shard, axis):
    length = lax.axis_size(axis)
    return lax.all_to_all(
        jnp.broadcast_to(shard[None], (length, *shard.shape)), axis, 0, 0, tiled=True
    )


def collect(shard, axis, dim):
    return in_order(sent_to_all(shard, axis), dim)


def upwind(padded, east_west, north_south):
    center = padded[:, 1:-1, 1:-1]
    western = padded[:, 1:-1, :-2]
    eastern = padded[:, 1:-1, 2:]
    southern = padded[:, :-2, 1:-1]
    northern = padded[:, 2:, 1:-1]
    zonal = jnp.maximum(east_west, 0.0) * (center - western) + jnp.minimum(east_west, 0.0) * (
        eastern - center
    )
    meridional = jnp.maximum(north_south, 0.0) * (center - southern) + jnp.minimum(
        north_south, 0.0
    ) * (northern - center)
    return center - zonal - meridional


def lon_rim(values, width):
    return padded_2(values, (("lat", 2),), width, True)


def lat_rim(values, width):
    return padded_2(values, (("mem", 1),), width, False)


def evolve(current, courant):
    fields = current.shape[0]
    stacked = jnp.concatenate([current, courant], axis=0)
    extended = lat_rim(lon_rim(stacked, STEPS), STEPS)
    result = extended[:fields]
    wind_ext = extended[fields:]
    for step_index in range(STEPS):
        margin = step_index + 1
        inner_wind = wind_ext[
            :, margin : wind_ext.shape[1] - margin, margin : wind_ext.shape[2] - margin
        ]
        result = upwind(result, inner_wind[0], inner_wind[1])
    return result


def per_device(control, perturb, lon_loc, lat_loc, static_scale, static_field, courant):
    along_lon = jnp.einsum(
        "mfal,lc->amfc",
        control,
        lax.all_gather(lon_loc, "mem", axis=1, tiled=True),
        preferred_element_type=jnp.float32,
    ).astype(jnp.bfloat16)
    banded = lax.all_to_all(along_lon, "lat", split_axis=3, concat_axis=0, tiled=True)
    mem_here = banded.shape[1]
    fields = banded.shape[2]
    lon_width = banded.shape[3]
    flat_band = banded.reshape(banded.shape[0], mem_here * fields * lon_width)
    pert_rows = jnp.transpose(perturb, (2, 0, 1, 3))
    lat_weights_all = collect(lat_loc, "mem", 0)
    members = mem_here * lax.axis_size("mem")
    ens_scale = 1.0 / math.sqrt(members - 1)
    rows_own = NLAT // lax.axis_size("mem")
    localized = jnp.dot(lat_weights_all, flat_band, preferred_element_type=jnp.float32)
    localized = localized.reshape(NLAT, mem_here, fields, lon_width)
    ensemble_all = jnp.transpose(
        lax.psum(jnp.sum(localized * pert_rows.astype(jnp.float32), axis=1) * ens_scale, "mem"),
        (1, 0, 2),
    )
    offset = lax.axis_index("mem") * rows_own
    ensemble = lax.dynamic_slice_in_dim(ensemble_all, offset, rows_own, 1)
    increment = ensemble + static_scale * static_field
    evolved = evolve(increment, courant)
    return (increment, evolved)


def solution(mesh):
    placed = (
        P("mem", None, "lat", None),
        P("mem", None, None, "lat"),
        P(None, "mem"),
        P("mem", None),
        P(None, "mem", "lat"),
        P(None, "mem", "lat"),
        P(None, "mem", "lat"),
    )
    return jax.shard_map(
        per_device,
        mesh=mesh,
        in_specs=placed,
        out_specs=(P(None, "mem", "lat"), P(None, "mem", "lat")),
        check_vma=False,
    )
```

profile of v0, /device:TPU:1, one launch (start us, length us, event | category | flops | bytes accessed | tf_op | source)
XLA Modules:
  0.0 541.9 jit_solution(11255603198932027136)
XLA Ops:
  7.2 0.7 all-gather.3.cloned.1.call-update
  7.9 2.0 broadcast_in_dim.2
  9.9 14.0 %all-to-all-start.1 = ((bf16[16,44,704]{2,1,0:T(8,128)(2,1)}), bf16[16,44,704]{2,1,0:T(8,128)(2,1)S(1)}, u32[]{:S(2)}, u32[]{:S(2)}) async-start(bf16[16,44,704]{2,1,0:T(8,128)(2,1)} %broadcast_in_dim.2), calls=%async_computation.1 | async-start | bytes 2359296 | tf_op jit(solution)/shard_map/all_to_all | solution.py:33
  23.9 111.8 %all-gather.3.cloned.1.call-done = bf16[16,90,1440]{2,1,0:T(8,128)(2,1)} async-done(((bf16[1,90,1440]{2,1,0:T(8,128)(2,1)}), bf16[16,90,1440]{2,1,0:T(8,128)(2,1)}) %all-gather.3.cloned.1.call-update) | async-done | bytes 4147216 | tf_op jit(solution)/shard_map/all_gather | solution.py:84
  135.8 5.9 %reshape.20 = bf16[1440,1440,1,1]{1,0,2,3:T(8,128)(2,1)} reshape(bf16[16,90,1440]{2,1,0:T(8,128)(2,1)} %all-gather.3.cloned.1.call-done) | data formatting | bytes 8294400
  141.7 6.0 %fusion.6 = bf16[22,2,10,1440]{3,0,2,1:T(8,128)(2,1)} fusion(bf16[1440,1440,1,1]{1,0,2,3:T(8,128)(2,1)} %reshape.20, bf16[2,10,22,1440]{3,0,2,1:T(2,128)(2,1)S(1)} %copy-done), kind=kOutput, calls=%fused_computation.5 | convolution fusion | flops 1825401600 | bytes 6681600 | tf_op jit(solution)/shard_map/mfal,lc->amfc/dot_general | solution.py:81
  147.7 15.6 %copy.36 = bf16[22,2,10,1440]{0,1,2,3:T(2,128)(2,1)} copy(bf16[22,2,10,1440]{3,0,2,1:T(8,128)(2,1)} %fusion.6) | data formatting | bytes 2534400 | tf_op jit(solution)/shard_map/convert_element_type | solution.py:86
  163.3 11.0 %reshape.22 = bf16[32,2,9900]{2,1,0:T(2,128)(2,1)} reshape(bf16[1440,10,2,22]{3,2,1,0:T(2,128)(2,1)} %bitcast.62) | data formatting | bytes 2534400
  174.3 1.0 copy-done.1
  175.3 12.5 %all-to-all-start = ((bf16[32,2,9900]{2,1,0:T(2,128)(2,1)}), bf16[32,2,9900]{2,1,0:T(2,128)(2,1)S(1)}, u32[]{:S(2)}, u32[]{:S(2)}) async-start(bf16[32,2,9900]{2,1,0:T(2,128)(2,1)} %reshape.22), calls=%async_computation | async-start | bytes 2555904 | tf_op jit(solution)/shard_map/all_to_all | solution.py:87
  187.9 2.3 reshape.16
  190.2 44.9 %all-to-all-done = bf16[32,2,9900]{2,1,0:T(2,128)(2,1)S(1)} async-done(((bf16[32,2,9900]{2,1,0:T(2,128)(2,1)}), bf16[32,2,9900]{2,1,0:T(2,128)(2,1)S(1)}, u32[]{:S(2)}, u32[]{:S(2)}) %all-to-all-start) | async-done | bytes 1267232 | tf_op jit(solution)/shard_map/all_to_all | solution.py:87
  235.1 7.4 %reshape.23 = bf16[1440,10,2,22]{3,2,1,0:T(2,128)(2,1)} reshape(bf16[32,2,9900]{2,1,0:T(2,128)(2,1)S(1)} %all-to-all-done) | data formatting | bytes 2534400
  242.5 25.1 %copy.53 = bf16[22,2,10,32,45]{4,2,1,0,3:T(8,128)(2,1)} copy(bf16[22,2,10,32,45]{0,1,2,4,3:T(2,128)(2,1)} %bitcast.61) | data formatting | bytes 2534400 | tf_op jit(solution)/shard_map/all_to_all | solution.py:87
  267.6 7.9 %reshape.15 = bf16[704,900]{1,0:T(8,128)(2,1)S(1)} reshape(bf16[32,22,2,10,45]{4,3,2,1,0:T(8,128)(2,1)} %bitcast.63) | data formatting | bytes 2534400 | tf_op jit(solution)/shard_map/reshape | solution.py:91
  275.5 4.3 convolution_bitcast_fusion
  279.8 3.9 reshape.17
  283.7 2.5 fusion.2
  286.2 1.2 broadcast_multiply_fusion
  287.5 0.9 copy-done.3
  288.9 206.1 %all-reduce.2.cloned.1.call-done = f32[704,10,45]{0,2,1:T(8,128)} async-done(((f32[704,10,45]{0,2,1:T(8,128)}), f32[704,10,45]{0,2,1:T(8,128)}) %all-reduce.2.cloned.1.call-update) | async-done | bytes 1267216 | tf_op jit(solution)/shard_map/psum | solution.py:100
  495.0 1.2 bitcast_add_fusion
  496.2 8.1 %collective-permute-start = (f32[12,44,4]{1,2,0:T(4,128)S(1)}, f32[12,44,4]{1,2,0:T(4,128)S(1)}, u32[]{:S(2)}, u32[]{:S(2)}) collective-permute-start(f32[12,44,4]{1,2,0:T(4,128)S(1)} %get-tuple-element.26), channel_id=1, source_target_pairs={{0,1},{1,2},{2,3},{3,4},{4,5},{5,6},{6,7},{7,8},{8,9},{9,10},{10,1... | collective-permute-start | bytes 25352 | tf_op jit(solution)/shard_map/ppermute | solution.py:19
  504.4 10.1 %collective-permute-start.1 = (f32[12,44,4]{1,2,0:T(4,128)S(1)}, f32[12,44,4]{1,2,0:T(4,128)S(1)}, u32[]{:S(2)}, u32[]{:S(2)}) collective-permute-start(f32[12,44,4]{1,2,0:T(4,128)S(1)} %get-tuple-element.27), channel_id=1, source_target_pairs={{1,0},{2,1},{3,2},{4,3},{5,4},{6,5},{7,6},{8,7},{9,8},{10,9},{11,1... | collective-permute-start | bytes 25352 | tf_op jit(solution)/shard_map/ppermute | solution.py:20
  514.5 3.4 collective-permute-done.1
  518.2 4.9 collective-permute-start.2
  523.1 7.6 %collective-permute-start.3 = (f32[12,4,53]{1,2,0:T(8,128)S(1)}, f32[12,4,53]{1,2,0:T(8,128)S(1)}, u32[]{:S(2)}, u32[]{:S(2)}) collective-permute-start(f32[12,4,53]{1,2,0:T(8,128)S(1)} %get-tuple-element.25), channel_id=1, source_target_pairs={{32,0},{64,32},{96,64},{128,96},{160,128},{192,160},{224,192},{256... | collective-permute-start | bytes 30536 | tf_op jit(solution)/shard_map/ppermute | solution.py:20
  531.2 0.9 copy.49
  532.7 0.4 fusion.20
  533.1 0.4 fusion.12
  533.5 0.3 fusion.36
  534.2 0.9 copy.50
  (37 shorter events, 2.2 us)
Async XLA Ops:
  7.2 134.5 %copy-start = (bf16[2,10,22,1440]{3,0,2,1:T(2,128)(2,1)S(1)}, bf16[2,10,22,1440]{3,0,2,1:T(2,128)(2,1)}, u32[]{:S(2)}) copy-start(bf16[2,10,22,1440]{3,0,2,1:T(2,128)(2,1)} %param.7) | copy-start | bytes 3801604
  7.2 128.6 %all-gather.3.cloned.1.call-start = ((), (), s32[]{:S(2)}) async-start(), calls=%async_computation.3 | async-start | bytes 5013504 | tf_op jit(solution)/shard_map/all_gather | solution.py:84
  9.9 164.4 %all-to-all-start.1 = ((bf16[16,44,704]{2,1,0:T(8,128)(2,1)}), bf16[16,44,704]{2,1,0:T(8,128)(2,1)S(1)}, u32[]{:S(2)}, u32[]{:S(2)}) async-start(bf16[16,44,704]{2,1,0:T(8,128)(2,1)} %broadcast_in_dim.2), calls=%async_computation.1 | async-start | bytes 2359296 | tf_op jit(solution)/shard_map/all_to_all | solution.py:33
  174.3 1.0 copy-start.1
  175.3 59.7 %all-to-all-start = ((bf16[32,2,9900]{2,1,0:T(2,128)(2,1)}), bf16[32,2,9900]{2,1,0:T(2,128)(2,1)S(1)}, u32[]{:S(2)}, u32[]{:S(2)}) async-start(bf16[32,2,9900]{2,1,0:T(2,128)(2,1)} %reshape.22), calls=%async_computation | async-start | bytes 2555904 | tf_op jit(solution)/shard_map/all_to_all | solution.py:87
  187.8 307.2 %all-reduce.2.cloned.1.call-start = ((), (), s32[]{:S(2)}) async-start(), calls=%async_computation.2 | async-start | bytes 2949120 | tf_op jit(solution)/shard_map/psum | solution.py:100
  279.8 3.9 copy-start.2
  287.5 0.9 copy-start.3
  287.5 1.1 copy-start.4
  287.5 1.3 copy-start.5
  496.2 18.3 %collective-permute-start = (f32[12,44,4]{1,2,0:T(4,128)S(1)}, f32[12,44,4]{1,2,0:T(4,128)S(1)}, u32[]{:S(2)}, u32[]{:S(2)}) collective-permute-start(f32[12,44,4]{1,2,0:T(4,128)S(1)} %get-tuple-element.26), channel_id=1, source_target_pairs={{0,1},{1,2},{2,3},{3,4},{4,5},{5,6},{6,7},{7,8},{8,9},{9,10},{10,1... | collective-permute-start | bytes 25352 | tf_op jit(solution)/shard_map/ppermute | solution.py:19
  504.4 13.6 %collective-permute-start.1 = (f32[12,44,4]{1,2,0:T(4,128)S(1)}, f32[12,44,4]{1,2,0:T(4,128)S(1)}, u32[]{:S(2)}, u32[]{:S(2)}) collective-permute-start(f32[12,44,4]{1,2,0:T(4,128)S(1)} %get-tuple-element.27), channel_id=1, source_target_pairs={{1,0},{2,1},{3,2},{4,3},{5,4},{6,5},{7,6},{8,7},{9,8},{10,9},{11,1... | collective-permute-start | bytes 25352 | tf_op jit(solution)/shard_map/ppermute | solution.py:20
  518.2 13.9 %collective-permute-start.2 = (f32[12,4,53]{1,2,0:T(8,128)S(1)}, f32[12,4,53]{1,2,0:T(8,128)S(1)}, u32[]{:S(2)}, u32[]{:S(2)}) collective-permute-start(f32[12,4,53]{1,2,0:T(8,128)S(1)} %get-tuple-element.24), channel_id=1, source_target_pairs={{0,32},{32,64},{64,96},{96,128},{128,160},{160,192},{192,224},{224... | collective-permute-start | bytes 30536 | tf_op jit(solution)/shard_map/ppermute | solution.py:19
  523.1 8.9 %collective-permute-start.3 = (f32[12,4,53]{1,2,0:T(8,128)S(1)}, f32[12,4,53]{1,2,0:T(8,128)S(1)}, u32[]{:S(2)}, u32[]{:S(2)}) collective-permute-start(f32[12,4,53]{1,2,0:T(8,128)S(1)} %get-tuple-element.25), channel_id=1, source_target_pairs={{32,0},{64,32},{96,64},{128,96},{160,128},{192,160},{224,192},{256... | collective-permute-start | bytes 30536 | tf_op jit(solution)/shard_map/ppermute | solution.py:20
Sparse Core Ops, SparseCore 0:
  10.1 125.6 all-gather.2
  287.6 207.3 all-reduce.1
where the time goes:
time: 545 us; the launch traced here: 542 us
  waiting for transfers between devices  367 us (67%)
  local copies, waits for them, and re-layouts  86 us (16%)
  starting transfers between devices  57.4 us (11%)
  between operations  14.2 us (3%)
  matrix products  10.2 us (2%)
  other arithmetic  7.06 us (1%)
    psum x1, waiting for transfers between devices, per_device(): lax.psum(jnp.sum(localized * pert_rows.astype(jnp.float32), axis=1) * ens...  206 us
    all_gather x1, waiting for transfers between devices, per_device(): lax.all_gather(lon_loc, 'mem', axis=1, tiled=True)  112 us
    all_to_all x1, waiting for transfers between devices, per_device(): lax.all_to_all(along_lon, 'lat', split_axis=3, concat_axis=0, tiled=True)  44.9 us
    unnamed x20, local copies, waits for them, and re-layouts  28.6 us
    all_to_all x1, local copies, waits for them, and re-layouts, per_device(): lax.all_to_all(along_lon, 'lat', split_axis=3, concat_axis=0, tiled=True)  25.1 us
    ppermute x2, starting transfers between devices, padded_2(): after = lax.ppermute(leading, axis, down)  17.7 us
    convert_element_type x1, local copies, waits for them, and re-layouts, per_device(): along_lon = jnp.einsum('mfal,lc->amfc', control, lax.all_gather(lon_loc,...  15.6 us
    all_to_all x1, starting transfers between devices, sent_to_all(): lax.all_to_all(jnp.broadcast_to(shard[None], (length, *shard.shape)), axi...  14 us
  transfers between devices with their start and end apart: 8, of which 4 were waited for; matrix products, arithmetic and copies ran while one was open for 8% of the time, Pallas kernels for 0%

commit v1 on v0

v1 whole, which is shorter than its diff:
```python
import functools
import math

import jax
import jax.numpy as jnp
from jax import lax
from jax.experimental import pallas as pl
from jax.experimental.pallas import tpu as pltpu
from jax.sharding import PartitionSpec as P

STEPS = 4
ZLO = 8
CORES = 2
XY = 16
ZHI = 2
MEM = ZLO * CORES
LAT = XY * ZHI
FIELDS = 10
HALF = FIELDS // 2
LOCAL = 2
NLAT = 704
NLON = 1440
BAND = NLAT // LAT
BAND_PAD = 24
WIDTH = NLON // LAT
ROWS = NLAT // MEM
ROWS_EXT = ROWS + 2 * STEPS
ROWS_PAD = 56
LON_BLOCK = NLON // MEM
LAT_BLOCK = 2 * BAND_PAD
PACKED = LOCAL * HALF * WIDTH
SUMMED = HALF * WIDTH
EXPANDED = MEM * ROWS_PAD
MESH = pl.DeviceIdType.MESH
SCALE = 1.0 / math.sqrt(31.0)
NT = (((1,), (1,)), ((), ()))
NN = (((1,), (0,)), ((), ()))


def matmul(a, b, dims):
    return lax.dot_general(a, b, dims, preferred_element_type=jnp.float32)


def kernel(
    control_hbm, perturb_hbm, lon_hbm, lat_hbm, scale_ref, field_ref, courant_ref,
    inc_out, evo_out,
    control, members, lon_all, lat_all, packed, spread, expand, lat_t, pert_t,
    sum_send, sum_recv, rows_send, rows_recv, static_ext, wind, wind_send, wind_recv,
    state, edge_send, edge_recv,
    local_sem, up_send, up_recv, down_send, down_recv, twin_send, twin_recv,
    mem_send, mem_recv, pack_send, pack_recv, total_send, total_recv,
    rim_send, rim_recv, wind_ssem, wind_rsem, edge_ssem, edge_rsem,
):
    i = lax.axis_index("mem")
    j = lax.axis_index("lat")
    zl, c = i // 2, i % 2
    xy, h = j // 2, j % 2
    twin = 2 * zl + 1 - c
    above = (h * ZLO + zl + 1) % 16
    below = (h * ZLO + zl + 15) % 16

    def at(mem, lat):
        return {"mem": mem, "lat": lat}

    up_dev = at(2 * (above % ZLO) + c, 2 * xy + above // ZLO)
    down_dev = at(2 * (below % ZLO) + c, 2 * xy + below // ZLO)
    twin_dev = at(twin, j)

    def remote(src, dst, ssem, rsem, dev):
        return pltpu.make_async_remote_copy(
            src_ref=src, dst_ref=dst, send_sem=ssem, recv_sem=rsem,
            device_id=dev, device_id_type=MESH,
        )

    get_control = pltpu.make_async_copy(control_hbm, control, local_sem.at[0])
    get_lon = pltpu.make_async_copy(lon_hbm, lon_all.at[i], local_sem.at[1])
    get_lat = pltpu.make_async_copy(lat_hbm, lat_all.at[i], local_sem.at[2])
    get_members = pltpu.make_async_copy(perturb_hbm.at[c], members.at[c], local_sem.at[3])
    get_lon.start()
    get_control.start()
    get_lat.start()
    get_members.start()

    barrier = pltpu.get_barrier_semaphore()

    def greet(mem, lat):
        pl.semaphore_signal(barrier, inc=1, device_id=at(mem, lat), device_id_type=MESH)

    greet(2 * (above % ZLO) + c, 2 * xy + above // ZLO)
    greet(2 * (below % ZLO) + c, 2 * xy + below // ZLO)
    greet(twin, j)

    def greet_lat(k, carry):
        other = (j + k) % LAT
        greet(i, other)
        greet(twin, other)
        return carry

    lax.fori_loop(1, LAT, greet_lat, 0)

    def greet_mem(k, carry):
        other = (zl + k) % ZLO
        greet(2 * other, j)
        greet(2 * other + 1, j)
        return carry

    lax.fori_loop(1, ZLO, greet_mem, 0)
    pl.semaphore_wait(barrier, 3 + 2 * (LAT - 1) + 2 * (ZLO - 1))

    def pair(p, send, recv, slot, dev, first=False):
        lon_src = lon_hbm if first else lon_all.at[p]
        lat_src = lat_hbm if first else lat_all.at[p]
        return (
            remote(lon_src, lon_all.at[p], send.at[0, slot], recv.at[0, slot], dev),
            remote(lat_src, lat_all.at[p], send.at[1, slot], recv.at[1, slot], dev),
        )

    def start(copies):
        for copy in copies:
            copy.start()

    start(pair(i, up_send, up_recv, 0, up_dev, True))
    start(pair(i, down_send, down_recv, 0, down_dev, True))
    start(pair(i, twin_send, twin_recv, zl, twin_dev, True))

    product = scale_ref[...] * field_ref[...]
    static_ext[:, STEPS : STEPS + ROWS, :] = product
    rows_send[0, :FIELDS] = product[:, :8, :]
    rows_send[1, :FIELDS] = product[:, ROWS - 8 :, :]
    rows_send[0, FIELDS:] = courant_ref[:, :8, :]
    rows_send[1, FIELDS:] = courant_ref[:, ROWS - 8 :, :]
    first_row, last_row = i == 0, i == MEM - 1

    @pl.when(first_row)
    def _():
        rows_recv[0] = jnp.zeros(rows_recv.shape[1:], rows_recv.dtype)

    @pl.when(last_row)
    def _():
        rows_recv[1] = jnp.zeros(rows_recv.shape[1:], rows_recv.dtype)

    to_before = remote(rows_send.at[0], rows_recv.at[1], rim_send.at[0], rim_recv.at[1], at(jnp.maximum(i - 1, 0), j))
    to_after = remote(rows_send.at[1], rows_recv.at[0], rim_send.at[1], rim_recv.at[0], at(jnp.minimum(i + 1, MEM - 1), j))
    give_members = remote(
        perturb_hbm.at[1 - c], members.at[c], mem_send.at[0], mem_recv.at[0], twin_dev
    )

    get_lon.wait()
    get_control.wait()

    def relay(d):
        wait_from = pair((2 * ((zl + ZLO - d) % ZLO) + c), up_send, up_recv, d - 1, up_dev)
        for copy in wait_from:
            copy.wait_recv()
        p = 2 * ((zl + ZLO - d) % ZLO) + c
        if d < 4:
            start(pair(p, up_send, up_recv, d, up_dev))
        start(pair(p, twin_send, twin_recv, (zl + ZLO - d) % ZLO, twin_dev))
        if d < 4:
            q = 2 * ((zl + d) % ZLO) + c
            for copy in pair(q, down_send, down_recv, d - 1, down_dev):
                copy.wait_recv()
            if d < 3:
                start(pair(q, down_send, down_recv, d, down_dev))
            start(pair(q, twin_send, twin_recv, (zl + d) % ZLO, twin_dev))

    def block(n, carry):
        d = (n + 2) // 4
        r = (n + 2) % 4
        middle = (d + 3) // 4 - d // 4
        other = middle * (r // 2) + (1 - middle) * (r % 2)
        downward = middle * (r % 2)
        source = (zl + d * (2 * downward - 1) + ZLO) % ZLO
        p = 2 * source + (c + other) % 2

        @pl.when(n == 1)
        def _():
            relay(1)

        @pl.when(n == 4)
        def _():
            relay(2)

        @pl.when(n == 8)
        def _():
            relay(3)

        @pl.when(n == 12)
        def _():
            relay(4)

        @pl.when(other == 1)
        def _():
            for copy in pair(p, twin_send, twin_recv, source, twin_dev):
                copy.wait_recv()

        along = matmul(control[...], lon_all[p], NT)
        for hh in range(ZHI):
            for cc in range(CORES):
                pieces = [
                    along[
                        BAND_PAD * (m * FIELDS + cc * HALF + f) : BAND_PAD * (m * FIELDS + cc * HALF + f + 1),
                        WIDTH * hh : WIDTH * (hh + 1),
                    ]
                    for m in range(LOCAL)
                    for f in range(HALF)
                ]
                packed[p, hh, cc] = jnp.concatenate(pieces, axis=1).astype(jnp.bfloat16)
        for hh in range(ZHI):
            for cc in range(CORES):
                mine = jnp.logical_and(p == xy, jnp.logical_and(h == hh, c == cc))

                @pl.when(mine)
                def _():
                    pltpu.make_async_copy(packed.at[p, hh, cc], spread.at[c, j], pack_recv.at[c, j]).start()

                @pl.when(jnp.logical_not(mine))
                def _():
                    remote(
                        packed.at[p, hh, cc], spread.at[c, j],
                        pack_send.at[p, hh, cc], pack_recv.at[c, j],
                        at(2 * zl + cc, 2 * p + hh),
                    ).start()

        @pl.when(n == 1)
        def _():
            give_members.start()

            @pl.when(jnp.logical_not(first_row))
            def _():
                to_before.start()

            @pl.when(jnp.logical_not(last_row))
            def _():
                to_after.start()

        return carry

    lax.fori_loop(0, MEM, block, 0)

    @pl.when(jnp.logical_not(first_row))
    def _():
        to_after.wait_recv()
        to_before.wait_send()

    @pl.when(jnp.logical_not(last_row))
    def _():
        to_before.wait_recv()
        to_after.wait_send()

    static_ext[:, :STEPS, :] = rows_recv[0, :FIELDS, 8 - STEPS :, :]
    static_ext[:, STEPS + ROWS : ROWS_EXT, :] = rows_recv[1, :FIELDS, :STEPS, :]
    static_ext[:, ROWS_EXT:, :] = jnp.zeros((FIELDS, ROWS_PAD - ROWS_EXT, WIDTH), jnp.float32)
    wind[...] = jnp.zeros_like(wind)
    wind[:, :STEPS, STEPS : STEPS + WIDTH] = rows_recv[0, FIELDS:, 8 - STEPS :, :]
    wind[:, STEPS : STEPS + ROWS, STEPS : STEPS + WIDTH] = courant_ref[...]
    wind[:, STEPS + ROWS : ROWS_EXT, STEPS : STEPS + WIDTH] = rows_recv[1, FIELDS:, :STEPS, :]
    for side, low in enumerate((STEPS, WIDTH)):
        wind_send[side] = jnp.concatenate([wind[k, :, low : low + STEPS] for k in range(2)], axis=1)
    west, east = (j + LAT - 1) % LAT, (j + 1) % LAT
    wind_west = remote(wind_send.at[0], wind_recv.at[1], wind_ssem.at[0], wind_rsem.at[1], at(i, west))
    wind_east = remote(wind_send.at[1], wind_recv.at[0], wind_ssem.at[1], wind_rsem.at[0], at(i, east))
    wind_west.start()
    wind_east.start()

    def select_rows(k, carry):
        row = lax.broadcasted_iota(jnp.int32, (ROWS_PAD, NLAT), 0)
        col = lax.broadcasted_iota(jnp.int32, (ROWS_PAD, NLAT), 1)
        hit = jnp.logical_and(col == row + (ROWS * k - STEPS), row < ROWS_EXT)
        expand[k] = jnp.where(hit, 1.0, 0.0).astype(jnp.bfloat16)
        return carry

    lax.fori_loop(0, MEM, select_rows, 0)
    get_lat.wait()
    lat_flat = lat_all[...].reshape(MEM * LAT_BLOCK, NLAT)
    rows_half = EXPANDED // 2
    for part in range(2):
        chooser = expand[part * ZLO : (part + 1) * ZLO].reshape(rows_half, NLAT)
        lat_t[part] = matmul(chooser, lat_flat, NT).astype(jnp.bfloat16)
    get_members.wait()
    give_members.wait()
    for part in range(2):
        chooser = expand[part * ZLO : (part + 1) * ZLO].reshape(rows_half, NLAT)
        for s in range(CORES):
            pert_t[part, s] = matmul(chooser, members[s], NT).astype(jnp.bfloat16)

    wind_west.wait()
    wind_east.wait()
    for k in range(2):
        wind[k, :, :STEPS] = wind_recv[0, :, STEPS * k : STEPS * (k + 1)]
        wind[k, :, STEPS + WIDTH : 2 * STEPS + WIDTH] = wind_recv[1, :, STEPS * k : STEPS * (k + 1)]

    def arrived(k, carry):
        for s in range(CORES):
            remote(packed.at[0, 0, 0], spread.at[s, k], pack_send.at[0, 0, 0], pack_recv.at[s, k], twin_dev).wait_recv()
        return carry

    lax.fori_loop(0, LAT, arrived, 0)
    for part in range(2):
        total = None
        for s in range(CORES):
            term = matmul(lat_t[part], spread[s].reshape(LAT * BAND_PAD, PACKED), NN)
            term = term * pert_t[part, s].astype(jnp.float32)
            total = term if total is None else total + term
        summed = (total[:, :SUMMED] + total[:, SUMMED:]) * SCALE
        sum_send[part * ZLO : (part + 1) * ZLO] = summed.astype(jnp.bfloat16).reshape(ZLO, ROWS_PAD, SUMMED)

        def give(k, carry):
            owner = part * ZLO + k

            @pl.when(owner == i)
            def _():
                pltpu.make_async_copy(sum_send.at[owner], sum_recv.at[i], total_recv.at[i]).start()

            @pl.when(owner != i)
            def _():
                remote(sum_send.at[owner], sum_recv.at[i], total_send.at[owner], total_recv.at[i], at(owner, j)).start()

            return carry

        lax.fori_loop(0, ZLO, give, 0)

    def gathered(k, carry):
        remote(sum_send.at[0], sum_recv.at[k], total_send.at[0], total_recv.at[k], twin_dev).wait_recv()
        return carry

    lax.fori_loop(0, MEM, gathered, 0)
    state[...] = jnp.zeros_like(state)
    for s in range(CORES):
        ensemble = sum_recv[s].astype(jnp.float32)
        for z in range(1, ZLO):
            ensemble = ensemble + sum_recv[CORES * z + s].astype(jnp.float32)
        for f in range(HALF):
            field = ensemble[:, WIDTH * f : WIDTH * (f + 1)] + static_ext[s * HALF + f]
            state[s * HALF + f, :, STEPS : STEPS + WIDTH] = field
            inc_out[s * HALF + f] = field[STEPS : STEPS + ROWS, :]
    for side, low in enumerate((STEPS, WIDTH)):
        edge_send[side] = jnp.concatenate([state[f, :, low : low + STEPS] for f in range(FIELDS)], axis=1)
    edge_west = remote(edge_send.at[0], edge_recv.at[1], edge_ssem.at[0], edge_rsem.at[1], at(i, west))
    edge_east = remote(edge_send.at[1], edge_recv.at[0], edge_ssem.at[1], edge_rsem.at[0], at(i, east))
    edge_west.start()
    edge_east.start()

    for slot in range(4):
        for copy in pair(0, up_send, up_recv, slot, up_dev):
            copy.wait_send()
    for slot in range(3):
        for copy in pair(0, down_send, down_recv, slot, down_dev):
            copy.wait_send()

    def twins(k, carry):
        for copy in pair(0, twin_send, twin_recv, k, twin_dev):
            copy.wait_send()
        return carry

    lax.fori_loop(0, ZLO, twins, 0)

    def packs(p, carry):
        for hh in range(ZHI):
            for cc in range(CORES):
                mine = jnp.logical_and(p == xy, jnp.logical_and(h == hh, c == cc))

                @pl.when(jnp.logical_not(mine))
                def _():
                    remote(
                        packed.at[p, hh, cc], spread.at[0, 0], pack_send.at[p, hh, cc], pack_recv.at[0, 0], twin_dev
                    ).wait_send()

        return carry

    lax.fori_loop(0, MEM, packs, 0)

    def totals(k, carry):
        @pl.when(k != i)
        def _():
            remote(sum_send.at[k], sum_recv.at[0], total_send.at[k], total_recv.at[0], twin_dev).wait_send()

        return carry

    lax.fori_loop(0, MEM, totals, 0)

    edge_west.wait()
    edge_east.wait()
    u, v = wind[0], wind[1]
    u_pos, u_neg = jnp.maximum(u, 0.0), jnp.minimum(u, 0.0)
    v_pos, v_neg = jnp.maximum(v, 0.0), jnp.minimum(v, 0.0)
    for f in range(FIELDS):
        state[f, :, :STEPS] = edge_recv[0, :, STEPS * f : STEPS * (f + 1)]
        state[f, :, STEPS + WIDTH : 2 * STEPS + WIDTH] = edge_recv[1, :, STEPS * f : STEPS * (f + 1)]

    def advance(f, carry):
        q = state[f]
        for _ in range(STEPS):
            western = pltpu.roll(q, 1, 1)
            eastern = pltpu.roll(q, q.shape[1] - 1, 1)
            southern = pltpu.roll(q, 1, 0)
            northern = pltpu.roll(q, q.shape[0] - 1, 0)
            zonal = u_pos * (q - western) + u_neg * (eastern - q)
            meridional = v_pos * (q - southern) + v_neg * (northern - q)
            q = q - zonal - meridional
        evo_out[f] = q[STEPS : STEPS + ROWS, STEPS : STEPS + WIDTH]
        return carry

    lax.fori_loop(0, FIELDS, advance, 0)


def per_device(control, perturb, lon_loc, lat_loc, static_scale, static_field, courant):
    rows = jnp.pad(control, ((0, 0), (0, 0), (0, BAND_PAD - BAND), (0, 0)))
    rows = rows.reshape(LOCAL * FIELDS * BAND_PAD, NLON)
    halves = perturb.reshape(LOCAL, CORES, HALF, NLAT, WIDTH).transpose(1, 0, 2, 4, 3)
    halves = halves.reshape(CORES, PACKED, NLAT)
    lat_rows = jnp.pad(lat_loc.reshape(2, BAND, NLAT), ((0, 0), (0, BAND_PAD - BAND), (0, 0)))
    lat_rows = lat_rows.reshape(LAT_BLOCK, NLAT)
    anywhere = pl.BlockSpec(memory_space=pl.ANY)
    vmem = pl.BlockSpec(memory_space=pltpu.VMEM)
    bf16, f32 = jnp.bfloat16, jnp.float32
    dma = pltpu.SemaphoreType.DMA
    out = jax.ShapeDtypeStruct((FIELDS, ROWS, WIDTH), f32)
    return pl.pallas_call(
        kernel,
        out_shape=(out, out),
        in_specs=[anywhere] * 4 + [vmem] * 3,
        out_specs=(vmem, vmem),
        scratch_shapes=[
            pltpu.VMEM((LOCAL * FIELDS * BAND_PAD, NLON), bf16),
            pltpu.VMEM((CORES, PACKED, NLAT), bf16),
            pltpu.VMEM((MEM, LON_BLOCK, NLON), bf16),
            pltpu.VMEM((MEM, LAT_BLOCK, NLAT), bf16),
            pltpu.VMEM((XY, ZHI, CORES, BAND_PAD, PACKED), bf16),
            pltpu.VMEM((CORES, LAT, BAND_PAD, PACKED), bf16),
            pltpu.VMEM((MEM, ROWS_PAD, NLAT), bf16),
            pltpu.VMEM((2, EXPANDED // 2, LAT * BAND_PAD), bf16),
            pltpu.VMEM((2, CORES, EXPANDED // 2, PACKED), bf16),
            pltpu.VMEM((MEM, ROWS_PAD, SUMMED), bf16),
            pltpu.VMEM((MEM, ROWS_PAD, SUMMED), bf16),
            pltpu.VMEM((2, FIELDS + 2, 8, WIDTH), f32),
            pltpu.VMEM((2, FIELDS + 2, 8, WIDTH), f32),
            pltpu.VMEM((FIELDS, ROWS_PAD, WIDTH), f32),
            pltpu.VMEM((2, ROWS_PAD, 128), f32),
            pltpu.VMEM((2, ROWS_PAD, 2 * STEPS), f32),
            pltpu.VMEM((2, ROWS_PAD, 2 * STEPS), f32),
            pltpu.VMEM((FIELDS, ROWS_PAD, 128), f32),
            pltpu.VMEM((2, ROWS_PAD, FIELDS * STEPS), f32),
            pltpu.VMEM((2, ROWS_PAD, FIELDS * STEPS), f32),
            dma((4,)), dma((2, 4)), dma((2, 4)), dma((2, 3)), dma((2, 3)), dma((2, ZLO)), dma((2, ZLO)),
            dma((1,)), dma((1,)), dma((XY, ZHI, CORES)), dma((CORES, LAT)), dma((MEM,)), dma((MEM,)),
            dma((2,)), dma((2,)), dma((2,)), dma((2,)), dma((2,)), dma((2,)),
        ],
        compiler_params=pltpu.CompilerParams(
            collective_id=0, has_side_effects=True, vmem_limit_bytes=56 * 1024 * 1024
        ),
        name="increment",
    )(rows, halves, lon_loc.T, lat_rows, static_scale, static_field, courant)


def solution(mesh):
    placed = (
        P("mem", None, "lat", None),
        P("mem", None, None, "lat"),
        P(None, "mem"),
        P("mem", None),
        P(None, "mem", "lat"),
        P(None, "mem", "lat"),
        P(None, "mem", "lat"),
    )
    return jax.shard_map(
        per_device,
        mesh=mesh,
        in_specs=placed,
        out_specs=(P(None, "mem", "lat"), P(None, "mem", "lat")),
        check_vma=False,
    )
```

time: 545 us -> 187 us (0.34)
  waiting for transfers between devices: 367 us -> 0 us
  Pallas kernels: 0 us -> 176 us
  local copies, waits for them, and re-layouts: 86 us -> 10.3 us
  starting transfers between devices: 57.4 us -> 0 us
  between operations: 14.2 us -> 0.68 us
  matrix products: 10.2 us -> 0 us
  other arithmetic: 7.06 us -> 0 us
    psum x1 -> x0, waiting for transfers between devices: 206 us -> none  [per_device(): lax.psum(jnp.sum(localized * pert_rows.astype(jnp.float32), axis=1) * ens...]
    pallas_call x0 -> x1, Pallas kernels: none -> 176 us  [per_device(): pl.pallas_call(kernel, out_shape=(out, out), in_specs=[anywhere] * 4 + [v...]
    all_gather x1 -> x0, waiting for transfers between devices: 112 us -> none  [per_device(): lax.all_gather(lon_loc, 'mem', axis=1, tiled=True)]
    all_to_all x2 -> x0, waiting for transfers between devices: 44.9 us -> none  [the longest x1 44.9 us: per_device(): lax.all_to_all(along_lon, 'lat', split_axis=3, concat_axis=0, tiled=True)]
    ppermute x4 -> x0, starting transfers between devices: 30.8 us -> none  [the longest x2 17.7 us: padded_2(): after = lax.ppermute(leading, axis, down)]
    all_to_all x2 -> x0, starting transfers between devices: 26.5 us -> none  [the longest x1 14 us: sent_to_all(): lax.all_to_all(jnp.broadcast_to(shard[None], (length, *shard.shape)), axi...]
    all_to_all x1 -> x0, local copies, waits for them, and re-layouts: 25.1 us -> none  [per_device(): lax.all_to_all(along_lon, 'lat', split_axis=3, concat_axis=0, tiled=True)]
    unnamed x20 -> x10, local copies, waits for them, and re-layouts: 28.6 us -> 6.02 us
  transfers between devices with their start and end apart: 8 -> 0, of which waited for: 4 -> 0; matrix products, arithmetic and copies ran while one was open for 8% -> 0% of each run, Pallas kernels for 0% -> 0%
where the time goes in v1:
time: 187 us
  Pallas kernels  176 us (94%)
  local copies, waits for them, and re-layouts  10.3 us (6%)
    pallas_call x1, Pallas kernels, per_device(): pl.pallas_call(kernel, out_shape=(out, out), in_specs=[anywhere] * 4 + [v...  176 us
    unnamed x10, local copies, waits for them, and re-layouts  6.02 us

profile of v1, /device:TPU:1, one launch (start us, length us, event | category | flops | bytes accessed | tf_op | source)
XLA Modules:
  0.0 187.2 jit_solution(7768475887192359003)
XLA Ops:
  0.6 1.5 copy.16
  2.1 0.0 copy-start
  2.1 1.3 pad.8.clone
  3.4 0.6 copy-done
  4.0 1.1 copy.13
  5.1 0.0 copy-start.1
  5.1 0.0 copy-start.2
  5.1 1.3 copy.14.perturb_hbm
  6.4 0.0 copy-done.1
  6.4 0.6 pad.9
  7.0 0.0 copy-done.2
  7.0 0.6 copy.15.courant_ref
  7.7 176.2 %increment.1 = (f32[10,44,45]{2,1,0:T(8,128)}, f32[10,44,45]{2,1,0:T(8,128)}) custom-call(bf16[480,1440]{1,0:T(8,128)(2,1)} %bitcast.7, bf16[2,450,704]{2,1,0:T(8,128)(2,1)} %copy.14.perturb_hbm, bf16[90,1440]{1,0:T(8,128)(2,1)} %bitcast.10, bf16[48,704]{1,0:T(8,128)(2,1)} %bitcast.11, f32[10,44,45]{2,1,0:T(8,128)} %scale_ref.1, f32[10,44,45]{2,1,0:T(8,128)} %field_ref.1, ...), custom_call_target="tpu_custom_call" | custom-call | tf_op jit(solution)/shard_map/increment/pallas_call | solution.py:419
  183.9 1.7 copy.19
  185.5 1.7 copy.20
  (1 shorter events, 0.0 us)
Async XLA Ops:
  2.1 1.9 %copy-start = (bf16[2,10,704,45]{2,0,3,1:T(2,128)(2,1)S(1)}, bf16[2,10,704,45]{2,0,3,1:T(2,128)(2,1)}, u32[]{:S(2)}) copy-start(bf16[2,10,704,45]{2,0,3,1:T(2,128)(2,1)} %param.8) | copy-start | bytes 3801604
  5.1 1.3 copy-start.1
  5.1 2.0 %copy-start.2 = (f32[2,44,45]{2,0,1:T(2,128)S(1)}, f32[2,44,45]{2,0,1:T(2,128)}, u32[]{:S(2)}) copy-start(f32[2,44,45]{2,0,1:T(2,128)} %param.13) | copy-start | bytes 47524

commit v2 on v1

--- a/solution.py
+++ b/solution.py
@@ -28,6 +28,12 @@
 ROWS_PAD = 56
 LON_BLOCK = NLON // MEM
 LAT_BLOCK = 2 * BAND_PAD
+QUARTERS = 4
+LANES = 128
+WHOLE = 3 * LANES
+REST = LOCAL * HALF * WIDTH - WHOLE
+FOLD = LANES - REST
+WIRE_ROWS = 3 * BAND_PAD + 16
 PACKED = LOCAL * HALF * WIDTH
 SUMMED = HALF * WIDTH
 EXPANDED = MEM * ROWS_PAD
@@ -45,9 +51,9 @@
     control_hbm, perturb_hbm, lon_hbm, lat_hbm, scale_ref, field_ref, courant_ref,
     inc_out, evo_out,
     control, members, lon_all, lat_all, packed, spread, expand, lat_t, pert_t,
-    sum_send, sum_recv, rows_send, rows_recv, static_ext, wind, wind_send, wind_recv,
+    rest, sum_send, sum_recv, rows_send, rows_recv, static_ext, wind, wind_send, wind_recv,
     state, edge_send, edge_recv,
-    local_sem, up_send, up_recv, down_send, down_recv, twin_send, twin_recv,
+    local_sem, up_send, up_recv, down_send, down_recv, side_send, side_recv, twin_send, twin_recv,
     mem_send, mem_recv, pack_send, pack_recv, total_send, total_recv,
     rim_send, rim_recv, wind_ssem, wind_rsem, edge_ssem, edge_rsem,
 ):
@@ -55,6 +61,8 @@
     j = lax.axis_index("lat")
     zl, c = i // 2, i % 2
     xy, h = j // 2, j % 2
+    x, y = xy // 4, xy % 4
+    half = (x + y) % 2
     twin = 2 * zl + 1 - c
     above = (h * ZLO + zl + 1) % 16
     below = (h * ZLO + zl + 15) % 16
@@ -65,6 +73,8 @@
     up_dev = at(2 * (above % ZLO) + c, 2 * xy + above // ZLO)
     down_dev = at(2 * (below % ZLO) + c, 2 * xy + below // ZLO)
     twin_dev = at(twin, j)
+    plus_dev = at(i, 2 * (4 * ((x + 1 - c) % 4) + (y + c) % 4) + h)
+    minus_dev = at(i, 2 * (4 * ((x + 3 * (1 - c)) % 4) + (y + 3 * c) % 4) + h)
 
     def remote(src, dst, ssem, rsem, dev):
         return pltpu.make_async_remote_copy(
@@ -107,21 +117,38 @@
     lax.fori_loop(1, ZLO, greet_mem, 0)
     pl.semaphore_wait(barrier, 3 + 2 * (LAT - 1) + 2 * (ZLO - 1))
 
-    def pair(p, send, recv, slot, dev, first=False):
-        lon_src = lon_hbm if first else lon_all.at[p]
-        lat_src = lat_hbm if first else lat_all.at[p]
+    get_lon.wait()
+    get_lat.wait()
+
+    def ring(p, send, recv, slot, dev):
+        part = lon_all.at[p, pl.ds(2 * half, 2)]
         return (
-            remote(lon_src, lon_all.at[p], send.at[0, slot], recv.at[0, slot], dev),
-            remote(lat_src, lat_all.at[p], send.at[1, slot], recv.at[1, slot], dev),
+            remote(part, part, send.at[0, slot], recv.at[0, slot], dev),
+            remote(lat_all.at[p, half], lat_all.at[p, half], send.at[1, slot], recv.at[1, slot], dev),
+        )
+
+    def beside(p, mine, slot):
+        first, second = lon_all.at[p, 2 * mine], lon_all.at[p, 2 * mine + 1]
+        third = lat_all.at[p, mine]
+        return (
+            remote(first, first, side_send.at[0, slot], side_recv.at[0, slot], plus_dev),
+            remote(second, second, side_send.at[1, slot], side_recv.at[1, slot], minus_dev),
+            remote(third, third, side_send.at[2, slot], side_recv.at[2, slot], plus_dev),
+        )
+
+    def across(p, slot):
+        return (
+            remote(lon_all.at[p], lon_all.at[p], twin_send.at[0, slot], twin_recv.at[0, slot], twin_dev),
+            remote(lat_all.at[p], lat_all.at[p], twin_send.at[1, slot], twin_recv.at[1, slot], twin_dev),
         )
 
     def start(copies):
         for copy in copies:
             copy.start()
 
-    start(pair(i, up_send, up_recv, 0, up_dev, True))
-    start(pair(i, down_send, down_recv, 0, down_dev, True))
-    start(pair(i, twin_send, twin_recv, zl, twin_dev, True))
+    start(ring(i, up_send, up_recv, 0, up_dev))
+    start(ring(i, down_send, down_recv, 0, down_dev))
+    start(across(i, zl))
 
     product = scale_ref[...] * field_ref[...]
     static_ext[:, STEPS : STEPS + ROWS, :] = product
@@ -145,24 +172,29 @@
         perturb_hbm.at[1 - c], members.at[c], mem_send.at[0], mem_recv.at[0], twin_dev
     )
 
-    get_lon.wait()
     get_control.wait()
 
     def relay(d):
-        wait_from = pair((2 * ((zl + ZLO - d) % ZLO) + c), up_send, up_recv, d - 1, up_dev)
-        for copy in wait_from:
+        source = (zl + ZLO - d) % ZLO
+        for copy in ring(2 * source + c, up_send, up_recv, d - 1, up_dev):
             copy.wait_recv()
-        p = 2 * ((zl + ZLO - d) % ZLO) + c
         if d < 4:
-            start(pair(p, up_send, up_recv, d, up_dev))
-        start(pair(p, twin_send, twin_recv, (zl + ZLO - d) % ZLO, twin_dev))
+            start(ring(2 * source + c, up_send, up_recv, d, up_dev))
+        start(beside(2 * source + c, half, source))
         if d < 4:
-            q = 2 * ((zl + d) % ZLO) + c
-            for copy in pair(q, down_send, down_recv, d - 1, down_dev):
+            source = (zl + d) % ZLO
+            for copy in ring(2 * source + c, down_send, down_recv, d - 1, down_dev):
                 copy.wait_recv()
             if d < 3:
-                start(pair(q, down_send, down_recv, d, down_dev))
-            start(pair(q, twin_send, twin_recv, (zl + d) % ZLO, twin_dev))
+                start(ring(2 * source + c, down_send, down_recv, d, down_dev))
+            start(beside(2 * source + c, half, source))
+
+    def complete(d):
+        for step in (-1, 1) if d < 4 else (-1,):
+            source = (zl + ZLO + step * d) % ZLO
+            for copy in beside(2 * source + c, 1 - half, source):
+                copy.wait_recv()
+            start(across(2 * source + c, source))
 
     def block(n, carry):
         d = (n + 2) // 4
@@ -173,28 +205,24 @@
         source = (zl + d * (2 * downward - 1) + ZLO) % ZLO
         p = 2 * source + (c + other) % 2
 
-        @pl.when(n == 1)
-        def _():
-            relay(1)
-
-        @pl.when(n == 4)
-        def _():
-            relay(2)
-
-        @pl.when(n == 8)
-        def _():
-            relay(3)
-
-        @pl.when(n == 12)
-        def _():
-            relay(4)
+        for d in range(1, 5):
+
+            @pl.when(n == (1 if d == 1 else 4 * (d - 1)))
+            def _():
+                relay(d)
+
+            @pl.when(n == 4 * d - 2)
+            def _():
+                complete(d)
 
         @pl.when(other == 1)
         def _():
-            for copy in pair(p, twin_send, twin_recv, source, twin_dev):
+            for copy in across(p, source):
                 copy.wait_recv()
 
-        along = matmul(control[...], lon_all[p], NT)
+        lon_rows = lon_all[p].reshape(QUARTERS * BAND_PAD, NLON)
+        along = matmul(control[...], lon_rows, NT)
+        lane = lax.broadcasted_iota(jnp.int32, (8, LANES), 1)
         for hh in range(ZHI):
             for cc in range(CORES):
                 pieces = [
@@ -205,7 +233,23 @@
                     for m in range(LOCAL)
                     for f in range(HALF)
                 ]
-                packed[p, hh, cc] = jnp.concatenate(pieces, axis=1).astype(jnp.bfloat16)
+                pieces.append(jnp.zeros((BAND_PAD, FOLD), jnp.float32))
+                row = jnp.concatenate(pieces, axis=1)
+                last = row[:, WHOLE:]
+                low, middle_rows, high = last[:8], last[8:16], last[16:]
+                folded = jnp.concatenate(
+                    [
+                        jnp.where(lane < REST, low, pltpu.roll(high, REST, 1)),
+                        jnp.where(
+                            lane < REST,
+                            middle_rows,
+                            jnp.where(lane < 2 * REST - FOLD, pltpu.roll(high, REST - FOLD, 1), 0.0),
+                        ),
+                    ],
+                    axis=0,
+                )
+                wire = [row[:, LANES * t : LANES * (t + 1)] for t in range(3)] + [folded]
+                packed[p, hh, cc] = jnp.concatenate(wire, axis=0).astype(jnp.bfloat16)
         for hh in range(ZHI):
             for cc in range(CORES):
                 mine = jnp.logical_and(p == xy, jnp.logical_and(h == hh, c == cc))
@@ -271,7 +315,6 @@
         return carry
 
     lax.fori_loop(0, MEM, select_rows, 0)
-    get_lat.wait()
     lat_flat = lat_all[...].reshape(MEM * LAT_BLOCK, NLAT)
     rows_half = EXPANDED // 2
     for part in range(2):
@@ -290,16 +333,26 @@
         wind[k, :, :STEPS] = wind_recv[0, :, STEPS * k : STEPS * (k + 1)]
         wind[k, :, STEPS + WIDTH : 2 * STEPS + WIDTH] = wind_recv[1, :, STEPS * k : STEPS * (k + 1)]
 
+    lane = lax.broadcasted_iota(jnp.int32, (8, LANES), 1)
+
     def arrived(k, carry):
         for s in range(CORES):
             remote(packed.at[0, 0, 0], spread.at[s, k], pack_send.at[0, 0, 0], pack_recv.at[s, k], twin_dev).wait_recv()
+            folded = spread[s, k, 3 * BAND_PAD :, :].astype(jnp.float32)
+            low, middle_rows = folded[:8], folded[8:]
+            high = jnp.where(
+                lane < FOLD, pltpu.roll(low, FOLD, 1), pltpu.roll(middle_rows, LANES - REST + FOLD, 1)
+            )
+            rest[s, k] = jnp.concatenate([low, middle_rows, high], axis=0).astype(jnp.bfloat16)
         return carry
 
     lax.fori_loop(0, LAT, arrived, 0)
     for part in range(2):
         total = None
         for s in range(CORES):
-            term = matmul(lat_t[part], spread[s].reshape(LAT * BAND_PAD, PACKED), NN)
+            tiles = [spread[s, :, BAND_PAD * t : BAND_PAD * (t + 1), :] for t in range(3)] + [rest[s]]
+            tiles = [t.reshape(LAT * BAND_PAD, LANES) for t in tiles]
+            term = matmul(lat_t[part], jnp.concatenate(tiles, axis=1), NN)[:, :PACKED]
             term = term * pert_t[part, s].astype(jnp.float32)
             total = term if total is None else total + term
         summed = (total[:, :SUMMED] + total[:, SUMMED:]) * SCALE
@@ -342,15 +395,21 @@
     edge_east.start()
 
     for slot in range(4):
-        for copy in pair(0, up_send, up_recv, slot, up_dev):
+        for copy in ring(0, up_send, up_recv, slot, up_dev):
             copy.wait_send()
     for slot in range(3):
-        for copy in pair(0, down_send, down_recv, slot, down_dev):
+        for copy in ring(0, down_send, down_recv, slot, down_dev):
             copy.wait_send()
 
     def twins(k, carry):
-        for copy in pair(0, twin_send, twin_recv, k, twin_dev):
+        for copy in across(0, k):
             copy.wait_send()
+
+        @pl.when(k != zl)
+        def _():
+            for copy in beside(0, half, k):
+                copy.wait_send()
+
         return carry
 
     lax.fori_loop(0, ZLO, twins, 0)
@@ -410,7 +469,8 @@
     halves = perturb.reshape(LOCAL, CORES, HALF, NLAT, WIDTH).transpose(1, 0, 2, 4, 3)
     halves = halves.reshape(CORES, PACKED, NLAT)
     lat_rows = jnp.pad(lat_loc.reshape(2, BAND, NLAT), ((0, 0), (0, BAND_PAD - BAND), (0, 0)))
-    lat_rows = lat_rows.reshape(LAT_BLOCK, NLAT)
+    lon_rows = jnp.pad(lon_loc.T, ((0, QUARTERS * BAND_PAD - LON_BLOCK), (0, 0)))
+    lon_rows = lon_rows.reshape(QUARTERS, BAND_PAD, NLON)
     anywhere = pl.BlockSpec(memory_space=pl.ANY)
     vmem = pl.BlockSpec(memory_space=pltpu.VMEM)
     bf16, f32 = jnp.bfloat16, jnp.float32
@@ -424,13 +484,14 @@
         scratch_shapes=[
             pltpu.VMEM((LOCAL * FIELDS * BAND_PAD, NLON), bf16),
             pltpu.VMEM((CORES, PACKED, NLAT), bf16),
-            pltpu.VMEM((MEM, LON_BLOCK, NLON), bf16),
-            pltpu.VMEM((MEM, LAT_BLOCK, NLAT), bf16),
-            pltpu.VMEM((XY, ZHI, CORES, BAND_PAD, PACKED), bf16),
-            pltpu.VMEM((CORES, LAT, BAND_PAD, PACKED), bf16),
+            pltpu.VMEM((MEM, QUARTERS, BAND_PAD, NLON), bf16),
+            pltpu.VMEM((MEM, 2, BAND_PAD, NLAT), bf16),
+            pltpu.VMEM((XY, ZHI, CORES, WIRE_ROWS, LANES), bf16),
+            pltpu.VMEM((CORES, LAT, WIRE_ROWS, LANES), bf16),
             pltpu.VMEM((MEM, ROWS_PAD, NLAT), bf16),
             pltpu.VMEM((2, EXPANDED // 2, LAT * BAND_PAD), bf16),
             pltpu.VMEM((2, CORES, EXPANDED // 2, PACKED), bf16),
+            pltpu.VMEM((CORES, LAT, BAND_PAD, LANES), bf16),
             pltpu.VMEM((MEM, ROWS_PAD, SUMMED), bf16),
             pltpu.VMEM((MEM, ROWS_PAD, SUMMED), bf16),
             pltpu.VMEM((2, FIELDS + 2, 8, WIDTH), f32),
@@ -442,7 +503,8 @@
             pltpu.VMEM((FIELDS, ROWS_PAD, 128), f32),
             pltpu.VMEM((2, ROWS_PAD, FIELDS * STEPS), f32),
             pltpu.VMEM((2, ROWS_PAD, FIELDS * STEPS), f32),
-            dma((4,)), dma((2, 4)), dma((2, 4)), dma((2, 3)), dma((2, 3)), dma((2, ZLO)), dma((2, ZLO)),
+            dma((4,)), dma((2, 4)), dma((2, 4)), dma((2, 3)), dma((2, 3)), dma((3, ZLO)), dma((3, ZLO)),
+            dma((2, ZLO)), dma((2, ZLO)),
             dma((1,)), dma((1,)), dma((XY, ZHI, CORES)), dma((CORES, LAT)), dma((MEM,)), dma((MEM,)),
             dma((2,)), dma((2,)), dma((2,)), dma((2,)), dma((2,)), dma((2,)),
         ],
@@ -450,7 +512,7 @@
             collective_id=0, has_side_effects=True, vmem_limit_bytes=56 * 1024 * 1024
         ),
         name="increment",
-    )(rows, halves, lon_loc.T, lat_rows, static_scale, static_field, courant)
+    )(rows, halves, lon_rows, lat_rows, static_scale, static_field, courant)
 
 
 def solution(mesh):

time: 187 us -> 171 us (0.914)
  the two profiles are of different devices: /device:TPU:1 before, /device:TPU:193 now
where the time goes in v2:
time: 171 us
  Pallas kernels  159 us (93%)
  local copies, waits for them, and re-layouts  11.1 us (6%)
    pallas_call x1, Pallas kernels, per_device(): pl.pallas_call(kernel, out_shape=(out, out), in_specs=[anywhere] * 4 + [v...  159 us
    unnamed x12, local copies, waits for them, and re-layouts  6.03 us

profile of v2, /device:TPU:193, one launch (start us, length us, event | category | flops | bytes accessed | tf_op | source)
XLA Modules:
  0.0 171.0 jit_solution(15645354401347778684)
XLA Ops:
  0.6 1.5 copy.16
  2.1 0.0 copy-start
  2.1 1.3 pad.12.clone
  3.4 0.6 copy-done
  4.0 1.1 copy.13
  5.1 0.0 copy-start.1
  5.1 0.0 copy-start.2
  5.1 0.0 copy-start.3
  5.1 1.3 copy.14.perturb_hbm
  6.4 0.0 copy-done.1
  6.4 0.8 pad.13
  7.1 0.0 copy-done.2
  7.2 0.6 pad.14.lat_hbm
  7.8 0.0 copy-done.3
  7.8 0.6 copy.15.courant_ref
  8.4 159.2 %increment.1 = (f32[10,44,45]{2,1,0:T(8,128)}, f32[10,44,45]{2,1,0:T(8,128)}) custom-call(bf16[480,1440]{1,0:T(8,128)(2,1)} %bitcast.7, bf16[2,450,704]{2,1,0:T(8,128)(2,1)} %copy.14.perturb_hbm, bf16[4,24,1440]{2,1,0:T(8,128)(2,1)} %bitcast.10, bf16[2,24,704]{2,1,0:T(8,128)(2,1)} %pad.14.lat_hbm, f32[10,44,45]{2,1,0:T(8,128)} %scale_ref.1, ...), custom_call_target="tpu_custom_call" | custom-call | tf_op jit(solution)/shard_map/increment/pallas_call | solution.py:479
  167.7 1.7 copy.19
  169.3 1.7 copy.20
  (1 shorter events, 0.0 us)
Async XLA Ops:
  2.1 1.9 %copy-start = (bf16[2,10,704,45]{2,0,3,1:T(2,128)(2,1)S(1)}, bf16[2,10,704,45]{2,0,3,1:T(2,128)(2,1)}, u32[]{:S(2)}) copy-start(bf16[2,10,704,45]{2,0,3,1:T(2,128)(2,1)} %param.8) | copy-start | bytes 3801604
  5.1 1.3 copy-start.1
  5.1 2.0 %copy-start.2 = (bf16[44,704]{1,0:T(8,128)(2,1)S(1)}, bf16[44,704]{1,0:T(8,128)(2,1)}, u32[]{:S(2)}) copy-start(bf16[44,704]{1,0:T(8,128)(2,1)} %param.10) | copy-start | bytes 185860
  5.1 2.7 %copy-start.3 = (f32[2,44,45]{2,0,1:T(2,128)S(1)}, f32[2,44,45]{2,0,1:T(2,128)}, u32[]{:S(2)}) copy-start(f32[2,44,45]{2,0,1:T(2,128)} %param.13) | copy-start | bytes 47524

commit v3 on v2

--- a/solution.py
+++ b/solution.py
@@ -33,7 +33,8 @@
 WHOLE = 3 * LANES
 REST = LOCAL * HALF * WIDTH - WHOLE
 FOLD = LANES - REST
-WIRE_ROWS = 3 * BAND_PAD + 16
+WIRE_ROWS = 3 * BAND_PAD + 8
+SPARE = REST - FOLD
 PACKED = LOCAL * HALF * WIDTH
 SUMMED = HALF * WIDTH
 EXPANDED = MEM * ROWS_PAD
@@ -48,9 +49,9 @@
 
 
 def kernel(
-    control_hbm, perturb_hbm, lon_hbm, lat_hbm, scale_ref, field_ref, courant_ref,
+    control_hbm, perturb_hbm, lon_ref, lat_ref, scale_ref, field_ref, courant_ref,
     inc_out, evo_out,
-    control, members, lon_all, lat_all, packed, spread, expand, lat_t, pert_t,
+    control_raw, control, members_raw, members, gift, lon_all, lat_all, packed, spread, expand, lat_t, pert_t,
     rest, sum_send, sum_recv, rows_send, rows_recv, static_ext, wind, wind_send, wind_recv,
     state, edge_send, edge_recv,
     local_sem, up_send, up_recv, down_send, down_recv, side_send, side_recv, twin_send, twin_recv,
@@ -82,13 +83,9 @@
             device_id=dev, device_id_type=MESH,
         )
 
-    get_control = pltpu.make_async_copy(control_hbm, control, local_sem.at[0])
-    get_lon = pltpu.make_async_copy(lon_hbm, lon_all.at[i], local_sem.at[1])
-    get_lat = pltpu.make_async_copy(lat_hbm, lat_all.at[i], local_sem.at[2])
-    get_members = pltpu.make_async_copy(perturb_hbm.at[c], members.at[c], local_sem.at[3])
-    get_lon.start()
+    get_control = pltpu.make_async_copy(control_hbm, control_raw, local_sem.at[0])
+    get_members = pltpu.make_async_copy(perturb_hbm, members_raw, local_sem.at[1])
     get_control.start()
-    get_lat.start()
     get_members.start()
 
     barrier = pltpu.get_barrier_semaphore()
@@ -115,10 +112,18 @@
         return carry
 
     lax.fori_loop(1, ZLO, greet_mem, 0)
+    for q in range(QUARTERS):
+        held = lon_ref[BAND_PAD * q : min(BAND_PAD * (q + 1), LON_BLOCK), :].astype(jnp.float32)
+        if held.shape[0] < BAND_PAD:
+            held = jnp.concatenate([held, jnp.zeros((BAND_PAD - held.shape[0], NLON), jnp.float32)], axis=0)
+        lon_all[i, q] = held.astype(jnp.bfloat16)
+    lat_rows = lat_ref[...].astype(jnp.float32)
+    for b in range(2):
+        held = jnp.concatenate(
+            [lat_rows[BAND * b : BAND * (b + 1)], jnp.zeros((BAND_PAD - BAND, NLAT), jnp.float32)], axis=0
+        )
+        lat_all[i, b] = held.astype(jnp.bfloat16)
     pl.semaphore_wait(barrier, 3 + 2 * (LAT - 1) + 2 * (ZLO - 1))
-
-    get_lon.wait()
-    get_lat.wait()
 
     def ring(p, send, recv, slot, dev):
         part = lon_all.at[p, pl.ds(2 * half, 2)]
@@ -154,8 +159,9 @@
     static_ext[:, STEPS : STEPS + ROWS, :] = product
     rows_send[0, :FIELDS] = product[:, :8, :]
     rows_send[1, :FIELDS] = product[:, ROWS - 8 :, :]
-    rows_send[0, FIELDS:] = courant_ref[:, :8, :]
-    rows_send[1, FIELDS:] = courant_ref[:, ROWS - 8 :, :]
+    for k in range(2):
+        rows_send[0, FIELDS + k] = courant_ref[:8, k, :]
+        rows_send[1, FIELDS + k] = courant_ref[ROWS - 8 :, k, :]
     first_row, last_row = i == 0, i == MEM - 1
 
     @pl.when(first_row)
@@ -169,10 +175,19 @@
     to_before = remote(rows_send.at[0], rows_recv.at[1], rim_send.at[0], rim_recv.at[1], at(jnp.maximum(i - 1, 0), j))
     to_after = remote(rows_send.at[1], rows_recv.at[0], rim_send.at[1], rim_recv.at[0], at(jnp.minimum(i + 1, MEM - 1), j))
     give_members = remote(
-        perturb_hbm.at[1 - c], members.at[c], mem_send.at[0], mem_recv.at[0], twin_dev
+        gift, members.at[c], mem_send.at[0], mem_recv.at[0], twin_dev
     )
 
     get_control.wait()
+
+    def place(f, carry):
+        held = control_raw[f].astype(jnp.float32)
+        for m in range(LOCAL):
+            rows = jnp.concatenate([held[:, m, :], jnp.zeros((BAND_PAD - BAND, NLON), jnp.float32)], axis=0)
+            control[m * FIELDS + f] = rows.astype(jnp.bfloat16)
+        return carry
+
+    lax.fori_loop(0, FIELDS, place, 0)
 
     def relay(d):
         source = (zl + ZLO - d) % ZLO
@@ -221,8 +236,9 @@
                 copy.wait_recv()
 
         lon_rows = lon_all[p].reshape(QUARTERS * BAND_PAD, NLON)
-        along = matmul(control[...], lon_rows, NT)
+        along = matmul(control[...].reshape(LOCAL * FIELDS * BAND_PAD, NLON), lon_rows, NT)
         lane = lax.broadcasted_iota(jnp.int32, (8, LANES), 1)
+        sub = lax.broadcasted_iota(jnp.int32, (8, LANES), 0)
         for hh in range(ZHI):
             for cc in range(CORES):
                 pieces = [
@@ -237,18 +253,19 @@
                 row = jnp.concatenate(pieces, axis=1)
                 last = row[:, WHOLE:]
                 low, middle_rows, high = last[:8], last[8:16], last[16:]
-                folded = jnp.concatenate(
-                    [
-                        jnp.where(lane < REST, low, pltpu.roll(high, REST, 1)),
-                        jnp.where(
-                            lane < REST,
-                            middle_rows,
-                            jnp.where(lane < 2 * REST - FOLD, pltpu.roll(high, REST - FOLD, 1), 0.0),
-                        ),
-                    ],
-                    axis=0,
-                )
-                wire = [row[:, LANES * t : LANES * (t + 1)] for t in range(3)] + [folded]
+                folded = jnp.where(lane < REST, low, pltpu.roll(middle_rows, REST, 1))
+                wire = []
+                for t in range(3):
+                    tile = row[:, LANES * t : LANES * (t + 1)]
+                    spare = jnp.where(lane < REST, pltpu.roll(high, 6 - 2 * t, 0), 0.0)
+                    if t == 0:
+                        for e in range(4):
+                            start_lane = REST + SPARE * e
+                            moved = pltpu.roll(pltpu.roll(middle_rows, start_lane - FOLD, 1), (6 - 2 * e) % 8, 0)
+                            inside = jnp.logical_and(lane >= start_lane, lane < start_lane + SPARE)
+                            spare = jnp.where(inside, moved, spare)
+                    wire += [tile[:16], jnp.where(sub < 6, tile[16:], spare)]
+                wire.append(folded)
                 packed[p, hh, cc] = jnp.concatenate(wire, axis=0).astype(jnp.bfloat16)
         for hh in range(ZHI):
             for cc in range(CORES):
@@ -268,8 +285,6 @@
 
         @pl.when(n == 1)
         def _():
-            give_members.start()
-
             @pl.when(jnp.logical_not(first_row))
             def _():
                 to_before.start()
@@ -281,6 +296,16 @@
         return carry
 
     lax.fori_loop(0, MEM, block, 0)
+
+    get_members.wait()
+
+    def member_rows(part):
+        rows = [members_raw[part * HALF + f].astype(jnp.float32)[:, m, :] for m in range(LOCAL) for f in range(HALF)]
+        return jnp.concatenate(rows, axis=0).astype(jnp.bfloat16)
+
+    gift[...] = member_rows(1 - c)
+    give_members.start()
+    members[c] = member_rows(c)
 
     @pl.when(jnp.logical_not(first_row))
     def _():
@@ -297,7 +322,8 @@
     static_ext[:, ROWS_EXT:, :] = jnp.zeros((FIELDS, ROWS_PAD - ROWS_EXT, WIDTH), jnp.float32)
     wind[...] = jnp.zeros_like(wind)
     wind[:, :STEPS, STEPS : STEPS + WIDTH] = rows_recv[0, FIELDS:, 8 - STEPS :, :]
-    wind[:, STEPS : STEPS + ROWS, STEPS : STEPS + WIDTH] = courant_ref[...]
+    for k in range(2):
+        wind[k, STEPS : STEPS + ROWS, STEPS : STEPS + WIDTH] = courant_ref[:, k, :]
     wind[:, STEPS + ROWS : ROWS_EXT, STEPS : STEPS + WIDTH] = rows_recv[1, FIELDS:, :STEPS, :]
     for side, low in enumerate((STEPS, WIDTH)):
         wind_send[side] = jnp.concatenate([wind[k, :, low : low + STEPS] for k in range(2)], axis=1)
@@ -320,7 +346,6 @@
     for part in range(2):
         chooser = expand[part * ZLO : (part + 1) * ZLO].reshape(rows_half, NLAT)
         lat_t[part] = matmul(chooser, lat_flat, NT).astype(jnp.bfloat16)
-    get_members.wait()
     give_members.wait()
     for part in range(2):
         chooser = expand[part * ZLO : (part + 1) * ZLO].reshape(rows_half, NLAT)
@@ -334,16 +359,25 @@
         wind[k, :, STEPS + WIDTH : 2 * STEPS + WIDTH] = wind_recv[1, :, STEPS * k : STEPS * (k + 1)]
 
     lane = lax.broadcasted_iota(jnp.int32, (8, LANES), 1)
+    sub = lax.broadcasted_iota(jnp.int32, (8, LANES), 0)
 
     def arrived(k, carry):
         for s in range(CORES):
             remote(packed.at[0, 0, 0], spread.at[s, k], pack_send.at[0, 0, 0], pack_recv.at[s, k], twin_dev).wait_recv()
             folded = spread[s, k, 3 * BAND_PAD :, :].astype(jnp.float32)
-            low, middle_rows = folded[:8], folded[8:]
-            high = jnp.where(
-                lane < FOLD, pltpu.roll(low, FOLD, 1), pltpu.roll(middle_rows, LANES - REST + FOLD, 1)
-            )
-            rest[s, k] = jnp.concatenate([low, middle_rows, high], axis=0).astype(jnp.bfloat16)
+            middle_rows = pltpu.roll(folded, FOLD, 1)
+            high = jnp.zeros((8, LANES), jnp.float32)
+            for t in range(3):
+                spare = spread[s, k, BAND_PAD * t + 16 : BAND_PAD * (t + 1), :].astype(jnp.float32)
+                pair = jnp.logical_and(sub >= 2 * t, sub < 2 * t + 2)
+                high = jnp.where(pair, pltpu.roll(spare, (2 * t + 2) % 8, 0), high)
+                if t == 0:
+                    for e in range(4):
+                        shift = (FOLD - REST - SPARE * e) % LANES
+                        moved = pltpu.roll(pltpu.roll(spare, shift, 1), (2 * e + 2) % 8, 0)
+                        inside = jnp.logical_and(sub >= 2 * e, sub < 2 * e + 2)
+                        middle_rows = jnp.where(jnp.logical_and(inside, lane >= FOLD), moved, middle_rows)
+            rest[s, k] = jnp.concatenate([folded, middle_rows, high], axis=0).astype(jnp.bfloat16)
         return carry
 
     lax.fori_loop(0, LAT, arrived, 0)
@@ -464,13 +498,6 @@
 
 
 def per_device(control, perturb, lon_loc, lat_loc, static_scale, static_field, courant):
-    rows = jnp.pad(control, ((0, 0), (0, 0), (0, BAND_PAD - BAND), (0, 0)))
-    rows = rows.reshape(LOCAL * FIELDS * BAND_PAD, NLON)
-    halves = perturb.reshape(LOCAL, CORES, HALF, NLAT, WIDTH).transpose(1, 0, 2, 4, 3)
-    halves = halves.reshape(CORES, PACKED, NLAT)
-    lat_rows = jnp.pad(lat_loc.reshape(2, BAND, NLAT), ((0, 0), (0, BAND_PAD - BAND), (0, 0)))
-    lon_rows = jnp.pad(lon_loc.T, ((0, QUARTERS * BAND_PAD - LON_BLOCK), (0, 0)))
-    lon_rows = lon_rows.reshape(QUARTERS, BAND_PAD, NLON)
     anywhere = pl.BlockSpec(memory_space=pl.ANY)
     vmem = pl.BlockSpec(memory_space=pltpu.VMEM)
     bf16, f32 = jnp.bfloat16, jnp.float32
@@ -479,11 +506,14 @@
     return pl.pallas_call(
         kernel,
         out_shape=(out, out),
-        in_specs=[anywhere] * 4 + [vmem] * 3,
+        in_specs=[anywhere] * 2 + [vmem] * 5,
         out_specs=(vmem, vmem),
         scratch_shapes=[
-            pltpu.VMEM((LOCAL * FIELDS * BAND_PAD, NLON), bf16),
+            pltpu.VMEM((FIELDS, BAND, LOCAL, NLON), bf16),
+            pltpu.VMEM((LOCAL * FIELDS, BAND_PAD, NLON), bf16),
+            pltpu.VMEM((FIELDS, WIDTH, LOCAL, NLAT), bf16),
             pltpu.VMEM((CORES, PACKED, NLAT), bf16),
+            pltpu.VMEM((PACKED, NLAT), bf16),
             pltpu.VMEM((MEM, QUARTERS, BAND_PAD, NLON), bf16),
             pltpu.VMEM((MEM, 2, BAND_PAD, NLAT), bf16),
             pltpu.VMEM((XY, ZHI, CORES, WIRE_ROWS, LANES), bf16),
@@ -512,7 +542,15 @@
             collective_id=0, has_side_effects=True, vmem_limit_bytes=56 * 1024 * 1024
         ),
         name="increment",
-    )(rows, halves, lon_rows, lat_rows, static_scale, static_field, courant)
+    )(
+        control.transpose(1, 2, 0, 3),
+        perturb.transpose(1, 3, 0, 2),
+        lon_loc.T,
+        lat_loc,
+        static_scale,
+        static_field,
+        courant.transpose(1, 0, 2),
+    )
 
 
 def solution(mesh):

time: 171 us -> 158 us (0.924)
  the two profiles are of different devices: /device:TPU:193 before, /device:TPU:1 now
where the time goes in v3:
time: 158 us; the launch traced here: 156 us
  Pallas kernels  152 us (96%)
  local copies, waits for them, and re-layouts  3.31 us (2%)
    pallas_call x1, Pallas kernels, per_device(): pl.pallas_call(kernel, out_shape=(out, out), in_specs=[anywhere] * 2 + [v...  152 us
    unnamed x2, local copies, waits for them, and re-layouts  3.31 us

profile of v3, /device:TPU:1, one launch (start us, length us, event | category | flops | bytes accessed | tf_op | source)
XLA Modules:
  0.0 156.1 jit_solution(3217899268755937939)
XLA Ops:
  0.6 152.1 %increment.1 = (f32[10,44,45]{2,1,0:T(8,128)}, f32[10,44,45]{2,1,0:T(8,128)}) custom-call(bf16[10,22,2,1440]{3,2,1,0:T(2,128)(2,1)} %bitcast.5, bf16[10,45,2,704]{3,2,1,0:T(2,128)(2,1)} %bitcast.4, bf16[90,1440]{1,0:T(8,128)(2,1)} %bitcast.6, bf16[44,704]{1,0:T(8,128)(2,1)} %lat_ref.1, f32[10,44,45]{2,1,0:T(8,128)} %scale_ref.1, f32[10,44,45]{2,1,0:T(8,128)} %field_ref.1, ...), custom_call_target="tpu_custom_call" | custom-call | tf_op jit(solution)/shard_map/increment/pallas_call | solution.py:506
  152.8 1.7 %copy.11 = f32[10,44,45]{2,1,0:T(8,128)} copy(f32[10,44,45]{2,1,0:T(8,128)} %get-tuple-element.4) | data formatting | bytes 158400
  154.4 1.7 %copy.12 = f32[10,44,45]{2,1,0:T(8,128)} copy(f32[10,44,45]{2,1,0:T(8,128)} %get-tuple-element.5) | data formatting | bytes 158400

commit v4 on v3

--- a/solution.py
+++ b/solution.py
@@ -38,6 +38,9 @@
 PACKED = LOCAL * HALF * WIDTH
 SUMMED = HALF * WIDTH
 EXPANDED = MEM * ROWS_PAD
+RELAY_AT = (1, 4, 8, 12)
+COMPLETE_AT = (2, 6, 10, 14)
+LAT_AT = (5, 7, 11, 13)
 MESH = pl.DeviceIdType.MESH
 SCALE = 1.0 / math.sqrt(31.0)
 NT = (((1,), (1,)), ((), ()))
@@ -64,6 +67,10 @@
     xy, h = j // 2, j % 2
     x, y = xy // 4, xy % 4
     half = (x + y) % 2
+    quarter = 2 * (x % 2) + y % 2
+    quarter_x, quarter_y = 2 - 2 * (x % 2) + y % 2, 2 * (x % 2) + 1 - y % 2
+    lag = 1 + xy % 8
+    next_x, next_y = (x + 1 + 2 * c) % 4, (y + 1 + 2 * c) % 4
     twin = 2 * zl + 1 - c
     above = (h * ZLO + zl + 1) % 16
     below = (h * ZLO + zl + 15) % 16
@@ -74,8 +81,9 @@
     up_dev = at(2 * (above % ZLO) + c, 2 * xy + above // ZLO)
     down_dev = at(2 * (below % ZLO) + c, 2 * xy + below // ZLO)
     twin_dev = at(twin, j)
-    plus_dev = at(i, 2 * (4 * ((x + 1 - c) % 4) + (y + c) % 4) + h)
-    minus_dev = at(i, 2 * (4 * ((x + 3 * (1 - c)) % 4) + (y + 3 * c) % 4) + h)
+    x_dev = at(i, 2 * (4 * next_x + y) + h)
+    y_dev = at(i, 2 * (4 * x + next_y) + h)
+    diagonal_dev = at(i, 2 * (4 * next_x + next_y) + h)
 
     def remote(src, dst, ssem, rsem, dev):
         return pltpu.make_async_remote_copy(
@@ -126,34 +134,36 @@
     pl.semaphore_wait(barrier, 3 + 2 * (LAT - 1) + 2 * (ZLO - 1))
 
     def ring(p, send, recv, slot, dev):
-        part = lon_all.at[p, pl.ds(2 * half, 2)]
-        return (
-            remote(part, part, send.at[0, slot], recv.at[0, slot], dev),
-            remote(lat_all.at[p, half], lat_all.at[p, half], send.at[1, slot], recv.at[1, slot], dev),
-        )
-
-    def beside(p, mine, slot):
-        first, second = lon_all.at[p, 2 * mine], lon_all.at[p, 2 * mine + 1]
-        third = lat_all.at[p, mine]
-        return (
-            remote(first, first, side_send.at[0, slot], side_recv.at[0, slot], plus_dev),
-            remote(second, second, side_send.at[1, slot], side_recv.at[1, slot], minus_dev),
-            remote(third, third, side_send.at[2, slot], side_recv.at[2, slot], plus_dev),
-        )
+        part = lon_all.at[p, quarter]
+        return remote(part, part, send.at[0, slot], recv.at[0, slot], dev)
+
+    def lat_ring(p, send, recv, slot, dev):
+        part = lat_all.at[p, half]
+        return remote(part, part, send.at[1, slot], recv.at[1, slot], dev)
+
+    def beside(p, parts, slot):
+        return [
+            remote(lon_all.at[p, part], lon_all.at[p, part], side_send.at[k, slot], side_recv.at[k, slot], dev)
+            for k, (part, dev) in enumerate(zip(parts, (x_dev, y_dev, diagonal_dev)))
+        ]
+
+    def lat_beside(p, part, slot):
+        part = lat_all.at[p, part]
+        return remote(part, part, side_send.at[3, slot], side_recv.at[3, slot], x_dev)
 
     def across(p, slot):
-        return (
-            remote(lon_all.at[p], lon_all.at[p], twin_send.at[0, slot], twin_recv.at[0, slot], twin_dev),
-            remote(lat_all.at[p], lat_all.at[p], twin_send.at[1, slot], twin_recv.at[1, slot], twin_dev),
-        )
+        return remote(lon_all.at[p], lon_all.at[p], twin_send.at[0, slot], twin_recv.at[0, slot], twin_dev)
+
+    def lat_across(p, slot):
+        return remote(lat_all.at[p], lat_all.at[p], twin_send.at[1, slot], twin_recv.at[1, slot], twin_dev)
 
     def start(copies):
         for copy in copies:
             copy.start()
 
-    start(ring(i, up_send, up_recv, 0, up_dev))
-    start(ring(i, down_send, down_recv, 0, down_dev))
-    start(across(i, zl))
+    ring(i, up_send, up_recv, 0, up_dev).start()
+    ring(i, down_send, down_recv, 0, down_dev).start()
+    across(i, zl).start()
 
     product = scale_ref[...] * field_ref[...]
     static_ext[:, STEPS : STEPS + ROWS, :] = product
@@ -189,51 +199,76 @@
 
     lax.fori_loop(0, FIELDS, place, 0)
 
-    def relay(d):
+    def relay(d, ring, share):
         source = (zl + ZLO - d) % ZLO
-        for copy in ring(2 * source + c, up_send, up_recv, d - 1, up_dev):
-            copy.wait_recv()
+        ring(2 * source + c, up_send, up_recv, d - 1, up_dev).wait_recv()
         if d < 4:
-            start(ring(2 * source + c, up_send, up_recv, d, up_dev))
-        start(beside(2 * source + c, half, source))
+            ring(2 * source + c, up_send, up_recv, d, up_dev).start()
+        share(2 * source + c, source)
         if d < 4:
             source = (zl + d) % ZLO
-            for copy in ring(2 * source + c, down_send, down_recv, d - 1, down_dev):
-                copy.wait_recv()
+            ring(2 * source + c, down_send, down_recv, d - 1, down_dev).wait_recv()
             if d < 3:
-                start(ring(2 * source + c, down_send, down_recv, d, down_dev))
-            start(beside(2 * source + c, half, source))
+                ring(2 * source + c, down_send, down_recv, d, down_dev).start()
+            share(2 * source + c, source)
 
     def complete(d):
         for step in (-1, 1) if d < 4 else (-1,):
             source = (zl + ZLO + step * d) % ZLO
-            for copy in beside(2 * source + c, 1 - half, source):
+            for copy in beside(2 * source + c, (quarter_x, quarter_y, 3 - quarter), source):
                 copy.wait_recv()
-            start(across(2 * source + c, source))
-
-    def block(n, carry):
+            across(2 * source + c, source).start()
+
+    def chosen(n):
         d = (n + 2) // 4
         r = (n + 2) % 4
         middle = (d + 3) // 4 - d // 4
         other = middle * (r // 2) + (1 - middle) * (r % 2)
         downward = middle * (r % 2)
         source = (zl + d * (2 * downward - 1) + ZLO) % ZLO
-        p = 2 * source + (c + other) % 2
+        return 2 * source + (c + other) % 2, source, other
+
+    def near(n):
+        p, _, _ = chosen(n)
+        for cc in range(CORES):
+            mine = jnp.logical_and(p == xy, c == cc)
+
+            @pl.when(mine)
+            def _():
+                pltpu.make_async_copy(packed.at[p, h, cc], spread.at[c, j], pack_recv.at[c, j]).start()
+
+            @pl.when(jnp.logical_not(mine))
+            def _():
+                remote(
+                    packed.at[p, h, cc], spread.at[c, j], pack_send.at[p, h, cc], pack_recv.at[c, j],
+                    at(2 * zl + cc, 2 * p + h),
+                ).start()
+
+    def block(n, carry):
+        p, source, other = chosen(n)
 
         for d in range(1, 5):
 
-            @pl.when(n == (1 if d == 1 else 4 * (d - 1)))
-            def _():
-                relay(d)
-
-            @pl.when(n == 4 * d - 2)
+            @pl.when(n == RELAY_AT[d - 1])
+            def _():
+                relay(d, ring, lambda p, k: start(beside(p, (quarter, quarter, quarter), k)))
+
+            @pl.when(n == COMPLETE_AT[d - 1])
             def _():
                 complete(d)
+
+            @pl.when(n == LAT_AT[d - 1])
+            def _():
+                if d == 1:
+                    lat_ring(i, up_send, up_recv, 0, up_dev).start()
+                    lat_ring(i, down_send, down_recv, 0, down_dev).start()
+                    lat_across(i, zl).start()
+                else:
+                    relay(d - 1, lat_ring, lambda p, k: lat_beside(p, half, k).start())
 
         @pl.when(other == 1)
         def _():
-            for copy in across(p, source):
-                copy.wait_recv()
+            across(p, source).wait_recv()
 
         lon_rows = lon_all[p].reshape(QUARTERS * BAND_PAD, NLON)
         along = matmul(control[...].reshape(LOCAL * FIELDS * BAND_PAD, NLON), lon_rows, NT)
@@ -267,21 +302,15 @@
                     wire += [tile[:16], jnp.where(sub < 6, tile[16:], spare)]
                 wire.append(folded)
                 packed[p, hh, cc] = jnp.concatenate(wire, axis=0).astype(jnp.bfloat16)
-        for hh in range(ZHI):
-            for cc in range(CORES):
-                mine = jnp.logical_and(p == xy, jnp.logical_and(h == hh, c == cc))
-
-                @pl.when(mine)
-                def _():
-                    pltpu.make_async_copy(packed.at[p, hh, cc], spread.at[c, j], pack_recv.at[c, j]).start()
-
-                @pl.when(jnp.logical_not(mine))
-                def _():
-                    remote(
-                        packed.at[p, hh, cc], spread.at[c, j],
-                        pack_send.at[p, hh, cc], pack_recv.at[c, j],
-                        at(2 * zl + cc, 2 * p + hh),
-                    ).start()
+        for cc in range(CORES):
+            remote(
+                packed.at[p, 1 - h, cc], spread.at[c, j], pack_send.at[p, 1 - h, cc], pack_recv.at[c, j],
+                at(2 * zl + cc, 2 * p + 1 - h),
+            ).start()
+
+        @pl.when(n >= lag)
+        def _():
+            near(n - lag)
 
         @pl.when(n == 1)
         def _():
@@ -297,6 +326,13 @@
 
     lax.fori_loop(0, MEM, block, 0)
 
+    def late(k, carry):
+        near(MEM - lag + k)
+        return carry
+
+    lax.fori_loop(0, lag, late, 0)
+
+    relay(4, lat_ring, lambda p, k: lat_beside(p, half, k).start())
     get_members.wait()
 
     def member_rows(part):
@@ -341,6 +377,22 @@
         return carry
 
     lax.fori_loop(0, MEM, select_rows, 0)
+
+    def lat_complete(k, carry):
+        @pl.when(k != zl)
+        def _():
+            lat_beside(2 * k + c, 1 - half, k).wait_recv()
+            lat_across(2 * k + c, k).start()
+
+        return carry
+
+    lax.fori_loop(0, ZLO, lat_complete, 0)
+
+    def lat_arrived(k, carry):
+        lat_across(2 * k + 1 - c, k).wait_recv()
+        return carry
+
+    lax.fori_loop(0, ZLO, lat_arrived, 0)
     lat_flat = lat_all[...].reshape(MEM * LAT_BLOCK, NLAT)
     rows_half = EXPANDED // 2
     for part in range(2):
@@ -392,20 +444,23 @@
         summed = (total[:, :SUMMED] + total[:, SUMMED:]) * SCALE
         sum_send[part * ZLO : (part + 1) * ZLO] = summed.astype(jnp.bfloat16).reshape(ZLO, ROWS_PAD, SUMMED)
 
-        def give(k, carry):
-            owner = part * ZLO + k
-
-            @pl.when(owner == i)
-            def _():
-                pltpu.make_async_copy(sum_send.at[owner], sum_recv.at[i], total_recv.at[i]).start()
-
-            @pl.when(owner != i)
-            def _():
-                remote(sum_send.at[owner], sum_recv.at[i], total_send.at[owner], total_recv.at[i], at(owner, j)).start()
-
-            return carry
-
-        lax.fori_loop(0, ZLO, give, 0)
+    def give(k, carry):
+        for step in (1, -1):
+            other = zl + step * (ZLO - 1 - k)
+
+            @pl.when(jnp.logical_and(other >= 0, other < ZLO))
+            def _():
+                for cc in range(CORES):
+                    owner = 2 * other + cc
+                    remote(
+                        sum_send.at[owner], sum_recv.at[i], total_send.at[owner], total_recv.at[i], at(owner, j)
+                    ).start()
+
+        return carry
+
+    lax.fori_loop(0, ZLO - 1, give, 0)
+    pltpu.make_async_copy(sum_send.at[i], sum_recv.at[i], total_recv.at[i]).start()
+    remote(sum_send.at[twin], sum_recv.at[i], total_send.at[twin], total_recv.at[i], twin_dev).start()
 
     def gathered(k, carry):
         remote(sum_send.at[0], sum_recv.at[k], total_send.at[0], total_recv.at[k], twin_dev).wait_recv()
@@ -428,21 +483,21 @@
     edge_west.start()
     edge_east.start()
 
-    for slot in range(4):
-        for copy in ring(0, up_send, up_recv, slot, up_dev):
-            copy.wait_send()
-    for slot in range(3):
-        for copy in ring(0, down_send, down_recv, slot, down_dev):
-            copy.wait_send()
+    for send in (ring, lat_ring):
+        for slot in range(4):
+            send(0, up_send, up_recv, slot, up_dev).wait_send()
+        for slot in range(3):
+            send(0, down_send, down_recv, slot, down_dev).wait_send()
 
     def twins(k, carry):
-        for copy in across(0, k):
-            copy.wait_send()
+        across(0, k).wait_send()
+        lat_across(0, k).wait_send()
 
         @pl.when(k != zl)
         def _():
-            for copy in beside(0, half, k):
+            for copy in beside(0, (quarter, quarter, quarter), k):
                 copy.wait_send()
+            lat_beside(0, half, k).wait_send()
 
         return carry
 
@@ -533,7 +588,7 @@
             pltpu.VMEM((FIELDS, ROWS_PAD, 128), f32),
             pltpu.VMEM((2, ROWS_PAD, FIELDS * STEPS), f32),
             pltpu.VMEM((2, ROWS_PAD, FIELDS * STEPS), f32),
-            dma((4,)), dma((2, 4)), dma((2, 4)), dma((2, 3)), dma((2, 3)), dma((3, ZLO)), dma((3, ZLO)),
+            dma((4,)), dma((2, 4)), dma((2, 4)), dma((2, 3)), dma((2, 3)), dma((4, ZLO)), dma((4, ZLO)),
             dma((2, ZLO)), dma((2, ZLO)),
             dma((1,)), dma((1,)), dma((XY, ZHI, CORES)), dma((CORES, LAT)), dma((MEM,)), dma((MEM,)),
             dma((2,)), dma((2,)), dma((2,)), dma((2,)), dma((2,)), dma((2,)),

time: 158 us -> 153 us (0.968)
  the two profiles are of different devices: /device:TPU:1 before, /device:TPU:97 now
where the time goes in v4:
time: 153 us
  Pallas kernels  149 us (97%)
  local copies, waits for them, and re-layouts  3.31 us (2%)
    pallas_call x1, Pallas kernels, per_device(): pl.pallas_call(kernel, out_shape=(out, out), in_specs=[anywhere] * 2 + [v...  149 us
    unnamed x2, local copies, waits for them, and re-layouts  3.31 us

profile of v4, /device:TPU:97, one launch (start us, length us, event | category | flops | bytes accessed | tf_op | source)
XLA Modules:
  0.0 152.6 jit_solution(16881671348800184021)
XLA Ops:
  0.6 148.6 %increment.1 = (f32[10,44,45]{2,1,0:T(8,128)}, f32[10,44,45]{2,1,0:T(8,128)}) custom-call(bf16[10,22,2,1440]{3,2,1,0:T(2,128)(2,1)} %bitcast.5, bf16[10,45,2,704]{3,2,1,0:T(2,128)(2,1)} %bitcast.4, bf16[90,1440]{1,0:T(8,128)(2,1)} %bitcast.6, bf16[44,704]{1,0:T(8,128)(2,1)} %lat_ref.1, f32[10,44,45]{2,1,0:T(8,128)} %scale_ref.1, f32[10,44,45]{2,1,0:T(8,128)} %field_ref.1, ...), custom_call_target="tpu_custom_call" | custom-call | tf_op jit(solution)/shard_map/increment/pallas_call | solution.py:561
  149.3 1.7 %copy.11 = f32[10,44,45]{2,1,0:T(8,128)} copy(f32[10,44,45]{2,1,0:T(8,128)} %get-tuple-element.4) | data formatting | bytes 158400
  150.9 1.7 %copy.12 = f32[10,44,45]{2,1,0:T(8,128)} copy(f32[10,44,45]{2,1,0:T(8,128)} %get-tuple-element.5) | data formatting | bytes 158400

commit v5 on v4

--- a/solution.py
+++ b/solution.py
@@ -35,6 +35,9 @@
 FOLD = LANES - REST
 WIRE_ROWS = 3 * BAND_PAD + 8
 SPARE = REST - FOLD
+SENT_ROWS = 48
+EDGE = HALF * WIDTH - LANES
+GAP = LANES - EDGE
 PACKED = LOCAL * HALF * WIDTH
 SUMMED = HALF * WIDTH
 EXPANDED = MEM * ROWS_PAD
@@ -131,40 +134,6 @@
             [lat_rows[BAND * b : BAND * (b + 1)], jnp.zeros((BAND_PAD - BAND, NLAT), jnp.float32)], axis=0
         )
         lat_all[i, b] = held.astype(jnp.bfloat16)
-    pl.semaphore_wait(barrier, 3 + 2 * (LAT - 1) + 2 * (ZLO - 1))
-
-    def ring(p, send, recv, slot, dev):
-        part = lon_all.at[p, quarter]
-        return remote(part, part, send.at[0, slot], recv.at[0, slot], dev)
-
-    def lat_ring(p, send, recv, slot, dev):
-        part = lat_all.at[p, half]
-        return remote(part, part, send.at[1, slot], recv.at[1, slot], dev)
-
-    def beside(p, parts, slot):
-        return [
-            remote(lon_all.at[p, part], lon_all.at[p, part], side_send.at[k, slot], side_recv.at[k, slot], dev)
-            for k, (part, dev) in enumerate(zip(parts, (x_dev, y_dev, diagonal_dev)))
-        ]
-
-    def lat_beside(p, part, slot):
-        part = lat_all.at[p, part]
-        return remote(part, part, side_send.at[3, slot], side_recv.at[3, slot], x_dev)
-
-    def across(p, slot):
-        return remote(lon_all.at[p], lon_all.at[p], twin_send.at[0, slot], twin_recv.at[0, slot], twin_dev)
-
-    def lat_across(p, slot):
-        return remote(lat_all.at[p], lat_all.at[p], twin_send.at[1, slot], twin_recv.at[1, slot], twin_dev)
-
-    def start(copies):
-        for copy in copies:
-            copy.start()
-
-    ring(i, up_send, up_recv, 0, up_dev).start()
-    ring(i, down_send, down_recv, 0, down_dev).start()
-    across(i, zl).start()
-
     product = scale_ref[...] * field_ref[...]
     static_ext[:, STEPS : STEPS + ROWS, :] = product
     rows_send[0, :FIELDS] = product[:, :8, :]
@@ -182,22 +151,56 @@
     def _():
         rows_recv[1] = jnp.zeros(rows_recv.shape[1:], rows_recv.dtype)
 
+    get_control.wait()
+
+    def place(f, carry):
+        held = control_raw[f].astype(jnp.float32)
+        for m in range(LOCAL):
+            rows = jnp.concatenate([held[:, m, :], jnp.zeros((BAND_PAD - BAND, NLON), jnp.float32)], axis=0)
+            control[m * FIELDS + f] = rows.astype(jnp.bfloat16)
+        return carry
+
+    lax.fori_loop(0, FIELDS, place, 0)
+
+    pl.semaphore_wait(barrier, 3 + 2 * (LAT - 1) + 2 * (ZLO - 1))
+
+    def ring(p, send, recv, slot, dev):
+        part = lon_all.at[p, quarter]
+        return remote(part, part, send.at[0, slot], recv.at[0, slot], dev)
+
+    def lat_ring(p, send, recv, slot, dev):
+        part = lat_all.at[p, half]
+        return remote(part, part, send.at[1, slot], recv.at[1, slot], dev)
+
+    def beside(p, parts, slot):
+        return [
+            remote(lon_all.at[p, part], lon_all.at[p, part], side_send.at[k, slot], side_recv.at[k, slot], dev)
+            for k, (part, dev) in enumerate(zip(parts, (x_dev, y_dev, diagonal_dev)))
+        ]
+
+    def lat_beside(p, part, slot):
+        part = lat_all.at[p, part]
+        return remote(part, part, side_send.at[3, slot], side_recv.at[3, slot], x_dev)
+
+    def across(p, slot):
+        return remote(lon_all.at[p], lon_all.at[p], twin_send.at[0, slot], twin_recv.at[0, slot], twin_dev)
+
+    def lat_across(p, slot):
+        return remote(lat_all.at[p], lat_all.at[p], twin_send.at[1, slot], twin_recv.at[1, slot], twin_dev)
+
+    def start(copies):
+        for copy in copies:
+            copy.start()
+
+    ring(i, up_send, up_recv, 0, up_dev).start()
+    ring(i, down_send, down_recv, 0, down_dev).start()
+    across(i, zl).start()
+
     to_before = remote(rows_send.at[0], rows_recv.at[1], rim_send.at[0], rim_recv.at[1], at(jnp.maximum(i - 1, 0), j))
     to_after = remote(rows_send.at[1], rows_recv.at[0], rim_send.at[1], rim_recv.at[0], at(jnp.minimum(i + 1, MEM - 1), j))
     give_members = remote(
         gift, members.at[c], mem_send.at[0], mem_recv.at[0], twin_dev
     )
-
-    get_control.wait()
-
-    def place(f, carry):
-        held = control_raw[f].astype(jnp.float32)
-        for m in range(LOCAL):
-            rows = jnp.concatenate([held[:, m, :], jnp.zeros((BAND_PAD - BAND, NLON), jnp.float32)], axis=0)
-            control[m * FIELDS + f] = rows.astype(jnp.bfloat16)
-        return carry
-
-    lax.fori_loop(0, FIELDS, place, 0)
 
     def relay(d, ring, share):
         source = (zl + ZLO - d) % ZLO
@@ -243,6 +246,44 @@
                     packed.at[p, h, cc], spread.at[c, j], pack_send.at[p, h, cc], pack_recv.at[c, j],
                     at(2 * zl + cc, 2 * p + h),
                 ).start()
+
+    west, east = (j + LAT - 1) % LAT, (j + 1) % LAT
+    wind_west = remote(wind_send.at[0], wind_recv.at[1], wind_ssem.at[0], wind_rsem.at[1], at(i, west))
+    wind_east = remote(wind_send.at[1], wind_recv.at[0], wind_ssem.at[1], wind_rsem.at[0], at(i, east))
+
+    def member_rows(part):
+        rows = [members_raw[part * HALF + f].astype(jnp.float32)[:, m, :] for m in range(LOCAL) for f in range(HALF)]
+        return jnp.concatenate(rows, axis=0).astype(jnp.bfloat16)
+
+    def share_members():
+        get_members.wait()
+        gift[...] = member_rows(1 - c)
+        give_members.start()
+        members[c] = member_rows(c)
+
+    def share_wind():
+        @pl.when(jnp.logical_not(first_row))
+        def _():
+            to_after.wait_recv()
+            to_before.wait_send()
+
+        @pl.when(jnp.logical_not(last_row))
+        def _():
+            to_before.wait_recv()
+            to_after.wait_send()
+
+        static_ext[:, :STEPS, :] = rows_recv[0, :FIELDS, 8 - STEPS :, :]
+        static_ext[:, STEPS + ROWS : ROWS_EXT, :] = rows_recv[1, :FIELDS, :STEPS, :]
+        static_ext[:, ROWS_EXT:, :] = jnp.zeros((FIELDS, ROWS_PAD - ROWS_EXT, WIDTH), jnp.float32)
+        wind[...] = jnp.zeros_like(wind)
+        wind[:, :STEPS, STEPS : STEPS + WIDTH] = rows_recv[0, FIELDS:, 8 - STEPS :, :]
+        for k in range(2):
+            wind[k, STEPS : STEPS + ROWS, STEPS : STEPS + WIDTH] = courant_ref[:, k, :]
+        wind[:, STEPS + ROWS : ROWS_EXT, STEPS : STEPS + WIDTH] = rows_recv[1, FIELDS:, :STEPS, :]
+        for side, low in enumerate((STEPS, WIDTH)):
+            wind_send[side] = jnp.concatenate([wind[k, :, low : low + STEPS] for k in range(2)], axis=1)
+        wind_west.start()
+        wind_east.start()
 
     def block(n, carry):
         p, source, other = chosen(n)
@@ -322,6 +363,14 @@
             def _():
                 to_after.start()
 
+        @pl.when(n == 9)
+        def _():
+            share_wind()
+
+        @pl.when(n == 11)
+        def _():
+            share_members()
+
         return carry
 
     lax.fori_loop(0, MEM, block, 0)
@@ -333,42 +382,6 @@
     lax.fori_loop(0, lag, late, 0)
 
     relay(4, lat_ring, lambda p, k: lat_beside(p, half, k).start())
-    get_members.wait()
-
-    def member_rows(part):
-        rows = [members_raw[part * HALF + f].astype(jnp.float32)[:, m, :] for m in range(LOCAL) for f in range(HALF)]
-        return jnp.concatenate(rows, axis=0).astype(jnp.bfloat16)
-
-    gift[...] = member_rows(1 - c)
-    give_members.start()
-    members[c] = member_rows(c)
-
-    @pl.when(jnp.logical_not(first_row))
-    def _():
-        to_after.wait_recv()
-        to_before.wait_send()
-
-    @pl.when(jnp.logical_not(last_row))
-    def _():
-        to_before.wait_recv()
-        to_after.wait_send()
-
-    static_ext[:, :STEPS, :] = rows_recv[0, :FIELDS, 8 - STEPS :, :]
-    static_ext[:, STEPS + ROWS : ROWS_EXT, :] = rows_recv[1, :FIELDS, :STEPS, :]
-    static_ext[:, ROWS_EXT:, :] = jnp.zeros((FIELDS, ROWS_PAD - ROWS_EXT, WIDTH), jnp.float32)
-    wind[...] = jnp.zeros_like(wind)
-    wind[:, :STEPS, STEPS : STEPS + WIDTH] = rows_recv[0, FIELDS:, 8 - STEPS :, :]
-    for k in range(2):
-        wind[k, STEPS : STEPS + ROWS, STEPS : STEPS + WIDTH] = courant_ref[:, k, :]
-    wind[:, STEPS + ROWS : ROWS_EXT, STEPS : STEPS + WIDTH] = rows_recv[1, FIELDS:, :STEPS, :]
-    for side, low in enumerate((STEPS, WIDTH)):
-        wind_send[side] = jnp.concatenate([wind[k, :, low : low + STEPS] for k in range(2)], axis=1)
-    west, east = (j + LAT - 1) % LAT, (j + 1) % LAT
-    wind_west = remote(wind_send.at[0], wind_recv.at[1], wind_ssem.at[0], wind_rsem.at[1], at(i, west))
-    wind_east = remote(wind_send.at[1], wind_recv.at[0], wind_ssem.at[1], wind_rsem.at[0], at(i, east))
-    wind_west.start()
-    wind_east.start()
-
     def select_rows(k, carry):
         row = lax.broadcasted_iota(jnp.int32, (ROWS_PAD, NLAT), 0)
         col = lax.broadcasted_iota(jnp.int32, (ROWS_PAD, NLAT), 1)
@@ -442,7 +455,29 @@
             term = term * pert_t[part, s].astype(jnp.float32)
             total = term if total is None else total + term
         summed = (total[:, :SUMMED] + total[:, SUMMED:]) * SCALE
-        sum_send[part * ZLO : (part + 1) * ZLO] = summed.astype(jnp.bfloat16).reshape(ZLO, ROWS_PAD, SUMMED)
+        summed = jnp.concatenate([summed, jnp.zeros((rows_half, GAP), jnp.float32)], axis=1)
+        for k in range(ZLO):
+            chunk = summed[ROWS_PAD * k : ROWS_PAD * (k + 1)]
+            right = chunk[:, LANES:]
+            left_end, right_end = chunk[SENT_ROWS:, :LANES], right[SENT_ROWS:]
+            strips = []
+            for t in range(SENT_ROWS // 8):
+                strip = right[8 * t : 8 * (t + 1)]
+                if t < 4:
+                    if t < 3:
+                        second = pltpu.roll(right_end, EDGE - GAP * t, 1)
+                    else:
+                        second = jnp.where(
+                            lane < EDGE + 4,
+                            pltpu.roll(left_end, EDGE + 4, 1),
+                            pltpu.roll(right_end, EDGE + 4 - 3 * GAP, 1),
+                        )
+                    first = pltpu.roll(left_end, (EDGE - GAP * t) % LANES, 1)
+                    spare = jnp.where(sub < 4, first, pltpu.roll(second, 4, 0))
+                    strip = jnp.where(lane < EDGE, strip, spare)
+                strips.append(strip)
+            sent = jnp.concatenate([chunk[:SENT_ROWS, :LANES], jnp.concatenate(strips, axis=0)], axis=1)
+            sum_send[part * ZLO + k] = sent.astype(jnp.bfloat16)
 
     def give(k, carry):
         for step in (1, -1):
@@ -472,6 +507,19 @@
         ensemble = sum_recv[s].astype(jnp.float32)
         for z in range(1, ZLO):
             ensemble = ensemble + sum_recv[CORES * z + s].astype(jnp.float32)
+        left_end = jnp.zeros((8, LANES), jnp.float32)
+        right_end = left_end
+        for t in range(4):
+            strip = ensemble[8 * t : 8 * (t + 1), LANES:]
+            swapped = pltpu.roll(strip, 4, 0)
+            inside = jnp.logical_and(lane >= GAP * t, lane < GAP * (t + 1))
+            left_end = jnp.where(inside, pltpu.roll(strip, (GAP * t - EDGE) % LANES, 1), left_end)
+            if t < 3:
+                right_end = jnp.where(inside, pltpu.roll(swapped, (GAP * t - EDGE) % LANES, 1), right_end)
+            else:
+                left_end = jnp.where(lane >= 4 * GAP, pltpu.roll(swapped, LANES - EDGE - 4, 1), left_end)
+                right_end = jnp.where(lane >= 3 * GAP, pltpu.roll(swapped, LANES + 3 * GAP - EDGE - 4, 1), right_end)
+        ensemble = jnp.concatenate([ensemble, jnp.concatenate([left_end, right_end], axis=1)], axis=0)
         for f in range(HALF):
             field = ensemble[:, WIDTH * f : WIDTH * (f + 1)] + static_ext[s * HALF + f]
             state[s * HALF + f, :, STEPS : STEPS + WIDTH] = field
@@ -577,8 +625,8 @@
             pltpu.VMEM((2, EXPANDED // 2, LAT * BAND_PAD), bf16),
             pltpu.VMEM((2, CORES, EXPANDED // 2, PACKED), bf16),
             pltpu.VMEM((CORES, LAT, BAND_PAD, LANES), bf16),
-            pltpu.VMEM((MEM, ROWS_PAD, SUMMED), bf16),
-            pltpu.VMEM((MEM, ROWS_PAD, SUMMED), bf16),
+            pltpu.VMEM((MEM, SENT_ROWS, 2 * LANES), bf16),
+            pltpu.VMEM((MEM, SENT_ROWS, 2 * LANES), bf16),
             pltpu.VMEM((2, FIELDS + 2, 8, WIDTH), f32),
             pltpu.VMEM((2, FIELDS + 2, 8, WIDTH), f32),
             pltpu.VMEM((FIELDS, ROWS_PAD, WIDTH), f32),

time: 153 us -> 149 us (0.974)
  the two profiles are of different devices: /device:TPU:97 before, /device:TPU:38 now
where the time goes in v5:
time: 149 us
  Pallas kernels  145 us (97%)
  local copies, waits for them, and re-layouts  3.31 us (2%)
    pallas_call x1, Pallas kernels, per_device(): pl.pallas_call(kernel, out_shape=(out, out), in_specs=[anywhere] * 2 + [v...  145 us
    unnamed x2, local copies, waits for them, and re-layouts  3.31 us

profile of v5, /device:TPU:38, one launch (start us, length us, event | category | flops | bytes accessed | tf_op | source)
XLA Modules:
  0.0 149.0 jit_solution(3585722601150654416)
XLA Ops:
  0.6 145.1 %increment.1 = (f32[10,44,45]{2,1,0:T(8,128)}, f32[10,44,45]{2,1,0:T(8,128)}) custom-call(bf16[10,22,2,1440]{3,2,1,0:T(2,128)(2,1)} %bitcast.5, bf16[10,45,2,704]{3,2,1,0:T(2,128)(2,1)} %bitcast.4, bf16[90,1440]{1,0:T(8,128)(2,1)} %bitcast.6, bf16[44,704]{1,0:T(8,128)(2,1)} %lat_ref.1, f32[10,44,45]{2,1,0:T(8,128)} %scale_ref.1, f32[10,44,45]{2,1,0:T(8,128)} %field_ref.1, ...), custom_call_target="tpu_custom_call" | custom-call | tf_op jit(solution)/shard_map/increment/pallas_call | solution.py:609
  145.7 1.7 %copy.11 = f32[10,44,45]{2,1,0:T(8,128)} copy(f32[10,44,45]{2,1,0:T(8,128)} %get-tuple-element.4) | data formatting | bytes 158400
  147.4 1.7 %copy.12 = f32[10,44,45]{2,1,0:T(8,128)} copy(f32[10,44,45]{2,1,0:T(8,128)} %get-tuple-element.5) | data formatting | bytes 158400

commit v6 on v5

--- a/solution.py
+++ b/solution.py
@@ -479,21 +479,22 @@
             sent = jnp.concatenate([chunk[:SENT_ROWS, :LANES], jnp.concatenate(strips, axis=0)], axis=1)
             sum_send[part * ZLO + k] = sent.astype(jnp.bfloat16)
 
-    def give(k, carry):
-        for step in (1, -1):
-            other = zl + step * (ZLO - 1 - k)
-
-            @pl.when(jnp.logical_and(other >= 0, other < ZLO))
-            def _():
-                for cc in range(CORES):
-                    owner = 2 * other + cc
-                    remote(
-                        sum_send.at[owner], sum_recv.at[i], total_send.at[owner], total_recv.at[i], at(owner, j)
-                    ).start()
-
-        return carry
-
-    lax.fori_loop(0, ZLO - 1, give, 0)
+        def give(k, carry):
+            for step in (1, -1):
+                other = zl + step * (ZLO - 1 - k)
+
+                @pl.when(jnp.logical_and(other >= part * (ZLO // 2), other < (part + 1) * (ZLO // 2)))
+                def _():
+                    for cc in range(CORES):
+                        owner = 2 * other + cc
+                        remote(
+                            sum_send.at[owner], sum_recv.at[i], total_send.at[owner], total_recv.at[i], at(owner, j)
+                        ).start()
+
+            return carry
+
+        lax.fori_loop(0, ZLO - 1, give, 0)
+
     pltpu.make_async_copy(sum_send.at[i], sum_recv.at[i], total_recv.at[i]).start()
     remote(sum_send.at[twin], sum_recv.at[i], total_send.at[twin], total_recv.at[i], twin_dev).start()
 

time: 149 us -> 145 us (0.973)
  the two profiles are of different devices: /device:TPU:38 before, /device:TPU:167 now
where the time goes in v6:
time: 145 us
  Pallas kernels  141 us (97%)
  local copies, waits for them, and re-layouts  3.31 us (2%)
    pallas_call x1, Pallas kernels, per_device(): pl.pallas_call(kernel, out_shape=(out, out), in_specs=[anywhere] * 2 + [v...  141 us
    unnamed x2, local copies, waits for them, and re-layouts  3.31 us

profile of v6, /device:TPU:167, one launch (start us, length us, event | category | flops | bytes accessed | tf_op | source)
XLA Modules:
  0.0 144.8 jit_solution(10432845044235532613)
XLA Ops:
  0.6 140.9 %increment.1 = (f32[10,44,45]{2,1,0:T(8,128)}, f32[10,44,45]{2,1,0:T(8,128)}) custom-call(bf16[10,22,2,1440]{3,2,1,0:T(2,128)(2,1)} %bitcast.5, bf16[10,45,2,704]{3,2,1,0:T(2,128)(2,1)} %bitcast.4, bf16[90,1440]{1,0:T(8,128)(2,1)} %bitcast.6, bf16[44,704]{1,0:T(8,128)(2,1)} %lat_ref.1, f32[10,44,45]{2,1,0:T(8,128)} %scale_ref.1, f32[10,44,45]{2,1,0:T(8,128)} %field_ref.1, ...), custom_call_target="tpu_custom_call" | custom-call | tf_op jit(solution)/shard_map/increment/pallas_call | solution.py:610
  141.5 1.7 %copy.11 = f32[10,44,45]{2,1,0:T(8,128)} copy(f32[10,44,45]{2,1,0:T(8,128)} %get-tuple-element.4) | data formatting | bytes 158400
  143.1 1.7 %copy.12 = f32[10,44,45]{2,1,0:T(8,128)} copy(f32[10,44,45]{2,1,0:T(8,128)} %get-tuple-element.5) | data formatting | bytes 158400
